TPU v7x, 32 devices: a whole 2x2x4 slice. The times are simulated.
32 devices in a mesh: groups: 2 (over y), seq: 16 (over z, x, core).
Axes of the slice: x: 2, y: 2, z: 4, core: 2. Of those that a mesh axis runs over, the one named last changes fastest.
Arguments:
- queries: bfloat16 [8192, 768], P(('groups', 'seq')), parts along dimension 0, may hold values from -30 to 30
- keys: bfloat16 [8192, 128], P(('groups', 'seq')), parts along dimension 0, may hold values from -14 to 14
- values: bfloat16 [8192, 128], P(('groups', 'seq')), parts along dimension 0, may hold values from -6 to 6
- span_ids: int32 [64], P(('groups', 'seq')), parts along dimension 0, may hold values from 0 to 31, each once
- lengths: int32 [16], P('groups'), parts along dimension 0, may hold values from 1 to 16, 32 in all
- page_dest: int32 [64], P('groups'), parts along dimension 0, may hold values from 0 to 31, each once
Outputs:
- context: bfloat16 [8192, 768], P(('groups', 'seq')), parts along dimension 0
- paged_kv: bfloat16 [64, 128, 256], P(('groups', 'seq')), parts along dimension 0
There are 2 independent parts, one for each index of `groups`. A program takes and returns all parts, laid end to end along the dimension named above; each array names one. Nothing has to cross between parts.
Inputs may be any that keep to these rules, and one draw needn't show every extreme that they name: `span_ids`: every packed span number appears once over the whole array. The lengths sum to 32, and one of them equals 16. `page_dest`: every page slot receives exactly one span.
All inputs are finite; a program needn't handle non-finite values.
Results may differ from a plain program's by a relative error of at most 0.012.
The roundings to bfloat16 on the way count: a program that leaves them out, or rounds other values in their place, can miss the bound.
Values may be sent and summed in bfloat16 or wider, within the bound.
No kernel may reach another device: no remote copies, remote signals or barrier semaphores. Data moves between devices by JAX's collectives and lax.ppermute only.
A program may use at most 128 MiB of HBM per device.

v0:
```python
import functools
import math

import jax
import jax.numpy as jnp
import numpy as np
from jax import lax
from jax.experimental import pallas as pl
from jax.experimental.pallas import tpu as pltpu
from jax.sharding import PartitionSpec as P


HD = 128
QH = 6
SPAN = 128
THETA = 1000000.0
NEG = -1e30
META = 8
SCALE = math.log2(math.e) / math.sqrt(HD)


def tables(spans):
    half = HD // 2
    freq = THETA ** (-(np.arange(half, dtype=np.float64) * 2.0 / HD))
    at = np.concatenate([SPAN * np.arange(spans), np.arange(SPAN)]).astype(np.float64)
    angle = at[:, None] * freq[None, :]
    cosine, sine = np.cos(angle), np.sin(angle)
    return (
        np.concatenate([cosine, cosine], axis=1).astype(np.float32),
        np.concatenate([-sine, sine], axis=1).astype(np.float32),
    )


def history(span, lengths_ref):
    start = jnp.int32(0)
    end = jnp.int32(0)
    for i in range(lengths_ref.shape[0]):
        end = end + lengths_ref[i]
        start = jnp.where(end <= span, end, start)
    return start


def turn(cos_ref, sin_ref, spans, depth):
    cos_a, sin_a = cos_ref[pl.ds(depth, 1), :], sin_ref[pl.ds(depth, 1), :]
    cos_b, sin_b = cos_ref[spans : spans + SPAN, :], sin_ref[spans : spans + SPAN, :]
    return cos_a * cos_b - sin_a * sin_b, sin_a * cos_b + cos_a * sin_b


def rotary(x, cosine, sine):
    x = x.astype(jnp.float32)
    return (x * cosine + pltpu.roll(x, HD // 2, 1) * sine).astype(jnp.bfloat16)


def fetch_all(pairs, sems):
    copies = [pltpu.make_async_copy(a, b, sems.at[i]) for i, (a, b) in enumerate(pairs)]
    for copy in copies:
        copy.start()
    return copies


def prepare(spans, *refs):
    out_ref = refs[6]
    ids_ref, lengths_ref, keys_ref, values_ref, cos_ref, sin_ref, sems = refs[7:]
    for copy in fetch_all(list(zip(refs[:6], refs[7:13])), sems):
        copy.wait()
    rows = keys_ref.shape[0]
    row = lax.broadcasted_iota(jnp.int32, (META, HD), 0)
    meta = jnp.zeros((META, HD), jnp.float32)
    for i in range(rows // SPAN):
        span = ids_ref[i]
        cosine, sine = turn(cos_ref, sin_ref, spans, span - history(span, lengths_ref))
        own = slice(i * SPAN, (i + 1) * SPAN)
        out_ref[own, :] = rotary(keys_ref[own, :], cosine, sine)
        meta = jnp.where(row == i, span.astype(jnp.float32), meta)
    out_ref[rows : 2 * rows, :] = values_ref[...]
    out_ref[2 * rows :, :] = meta.astype(jnp.bfloat16)


LADDER = (4, 2, 1)


def lanes(x, combine):
    parts = [x[:, i : i + HD] for i in range(0, x.shape[1], HD)]
    while len(parts) > 1:
        parts = [combine(*parts[i : i + 2]) if i + 1 < len(parts) else parts[i] for i in range(0, len(parts), 2)]
    return parts[0]


def scores_of(queries, keys):
    return lax.dot_general(
        queries, keys, (((1,), (1,)), ((), ())), preferred_element_type=jnp.float32
    )


def attend(queries, keys, values, old, old_total, old_accum, mask=None):
    scores = lax.dot_general(
        queries, keys, (((1,), (1,)), ((), ())), preferred_element_type=jnp.float32
    )
    if mask is not None:
        scores = jnp.where(mask, scores, NEG)
    top = jnp.max(lanes(scores, jnp.maximum), axis=1, keepdims=True)
    top = jnp.broadcast_to(top, (queries.shape[0], HD))
    if old is not None:
        top = jnp.maximum(old, top)
    weights = jnp.exp2((scores - jnp.tile(top, (1, keys.shape[0] // HD))) * SCALE)
    total = lanes(weights, jnp.add)
    accum = jnp.dot(weights.astype(jnp.bfloat16), values, preferred_element_type=jnp.float32)
    if old is not None:
        factor = jnp.exp2((old - top) * SCALE)
        total = total + old_total * factor
        accum = accum + old_accum * factor
    return top, total, accum


def early(spans, *refs):
    q_rot, best, total, accum = refs[6:10]
    ids_ref, lengths_ref, queries_ref, cos_ref, sin_ref, sems = refs[10:]
    own_ref = refs[5]
    for copy in fetch_all(list(zip(refs[:5], refs[10:15])), sems):
        copy.wait()
    tok = queries_ref.shape[0]
    rows = QH * SPAN
    row = lax.broadcasted_iota(jnp.int32, (rows, SPAN), 0) % SPAN
    key = lax.broadcasted_iota(jnp.int32, (rows, SPAN), 1)
    causal = key <= row
    for s in range(tok // SPAN):
        span = ids_ref[s]
        cosine, sine = turn(cos_ref, sin_ref, spans, span - history(span, lengths_ref))
        for h in range(QH):
            q_rot[s * rows + h * SPAN : s * rows + (h + 1) * SPAN, :] = rotary(
                queries_ref[s * SPAN : (s + 1) * SPAN, h * HD : (h + 1) * HD], cosine, sine
            )
        keys = own_ref[s * SPAN : (s + 1) * SPAN, :]
        values = own_ref[tok + s * SPAN : tok + (s + 1) * SPAN, :]
        own = slice(s * rows, (s + 1) * rows)
        best[own, :], total[own, :], accum[own, :] = attend(
            q_rot[own, :], keys, values, None, None, None, causal
        )


def absorb(
    per_rank, count, last, first_page_ref, ids_ref, lengths_ref, dest_ref, q_rot, best_in, total_in, accum_in, *rest
):
    pieces, rest = rest[:count], rest[count:]
    if last:
        _, context_ref, pages_ref, best, total, accum, rows_out = rest[:7]
        rest = rest[7:]
    else:
        best, total, accum, pages_ref = rest[:4]
        rest = rest[4:]
    kv, page, ids_vmem, where, ids_smem, id_sem, page_sem, out_sem = rest
    tok = per_rank * SPAN
    rows = QH * SPAN
    block = 2 * tok + META

    lane = lax.broadcasted_iota(jnp.int32, (META, HD), 1)
    blocks = [(p, base) for p in pieces for base in range(0, p.shape[0], block)]
    for group in range(ids_vmem.shape[0]):
        found = jnp.zeros((META, HD), jnp.float32)
        for i in range(group * HD, min((group + 1) * HD, len(blocks))):
            piece, base = blocks[i]
            meta = piece[base + 2 * tok : base + block, :].astype(jnp.float32)
            found = jnp.where(lane == i - group * HD, meta, found)
        ids_vmem[group] = found.astype(jnp.int32)
    fetch = pltpu.make_async_copy(ids_vmem, ids_smem, id_sem)
    fetch.start()

    for i, (piece, base) in enumerate(blocks):
        kv[2 * tok * i : 2 * tok * (i + 1), :] = piece[base : base + 2 * tok, :]
    best[...] = best_in[...]
    total[...] = total_in[...]
    accum[...] = accum_in[...]

    own_ids = [ids_ref[s] for s in range(per_rank)]
    starts = [history(span, lengths_ref) for span in own_ids]
    first_page = first_page_ref[0]
    fetch.wait()

    def note(i, found):
        found = list(found)
        for j in range(per_rank):
            number = ids_smem[i // HD, j, i % HD]
            place = (2 * i * per_rank + j) * SPAN
            for s in range(per_rank):
                where[s, found[s]] = place
                seen = (number >= starts[s]) & (number < own_ids[s])
                found[s] = found[s] + seen.astype(jnp.int32)
            to = dest_ref[number] - first_page
            for p in range(per_rank):
                found[per_rank + p] = jnp.where(to == p, place, found[per_rank + p])
        return tuple(found)

    found = (jnp.int32(0),) * per_rank + (jnp.int32(-1),) * per_rank
    found = lax.fori_loop(0, len(blocks), note, found, unroll=len(blocks) <= 16)

    def tile(place):
        return kv[pl.ds(pl.multiple_of(place, SPAN), SPAN), :]

    def page_copy(p):
        return pltpu.make_async_copy(page.at[p], pages_ref.at[p], page_sem.at[p])

    for p in range(per_rank):

        @pl.when(found[per_rank + p] >= 0)
        def _():
            page[p, :, :HD] = tile(found[per_rank + p])
            page[p, :, HD:] = tile(found[per_rank + p] + tok)
            page_copy(p).start()

    def step(s, places):
        keys = jnp.concatenate([tile(p) for p in places], axis=0)
        values = jnp.concatenate([tile(p + tok) for p in places], axis=0)
        own = slice(s * rows, (s + 1) * rows)
        scores = scores_of(q_rot[own, :], keys)
        old = best[own, :]
        top = jnp.maximum(old, jnp.max(scores, axis=1, keepdims=True))
        factor = jnp.exp2((old - top) * SCALE)
        weights = jnp.exp2((scores - jnp.tile(top, (1, len(places)))) * SCALE)
        best[own, :] = top
        total[own, :] = total[own, :] * factor + lanes(weights, jnp.add)
        accum[own, :] = accum[own, :] * factor + jnp.dot(
            weights.astype(jnp.bfloat16), values, preferred_element_type=jnp.float32
        )

    outs = []
    for s in range(per_rank):
        seen = found[s]

        @pl.loop(0, seen // LADDER[0])
        def _(b):
            step(s, [where[s, LADDER[0] * b + i] for i in range(LADDER[0])])

        for size in LADDER[1:]:

            @pl.when(seen % (2 * size) >= size)
            def _():
                base = seen // (2 * size) * (2 * size)
                step(s, [where[s, base + i] for i in range(size)])

        if last:
            own = slice(s * SPAN, (s + 1) * SPAN)
            for h in range(QH):
                part = slice(s * rows + h * SPAN, s * rows + (h + 1) * SPAN)
                rows_out[own, h * HD : (h + 1) * HD] = (
                    accum[part, :] / jnp.sum(total[part, :], axis=1, keepdims=True)
                ).astype(jnp.bfloat16)
            outs.append(pltpu.make_async_copy(rows_out.at[own, :], context_ref.at[own, :], out_sem.at[s]))
            outs[-1].start()

    for copy in outs:
        copy.wait()
    for p in range(per_rank):

        @pl.when(found[per_rank + p] >= 0)
        def _():
            page_copy(p).wait()


SMEM = pl.BlockSpec(memory_space=pltpu.SMEM)
VMEM = pl.BlockSpec(memory_space=pltpu.VMEM)
ANY = pl.BlockSpec(memory_space=pltpu.HBM)
LIMIT = pltpu.CompilerParams(vmem_limit_bytes=24 << 20)


def vmem(x):
    return pltpu.with_memory_space_constraint(x, pltpu.VMEM)


def hbm(x):
    return pltpu.with_memory_space_constraint(x, pltpu.HBM)


ROUTE = (
    ("A", "o", 8),
    ("B", "o", 4),
    ("X", "o", 2),
    ("co", "o", 1),
    ("BA", "A", 4),
    ("XB", "B", 2),
    ("XA", "A", 2),
    ("cX", "X", 1),
    ("cA", "A", 1),
    ("cB", "B", 1),
    ("XBA", "BA", 2),
    ("cBA", "BA", 1),
    ("cXB", "XB", 1),
    ("cXA", "XA", 1),
    ("cXBA", "XBA", 1),
)
SOON = ("o", "X", "B", "A", "BA", "co", "cX", "cB", "cA")
LATE = ("cBA", "XB", "XA", "cXB", "cXA", "XBA", "cXBA")


def on_device(ranks, queries, keys, values, span_ids, lengths, page_dest):
    return plan(ranks, queries, keys, values, span_ids, lengths, page_dest)


def plan(ranks, queries, keys, values, span_ids, lengths, page_dest):
    tok = queries.shape[0]
    per_rank = span_ids.shape[0]
    spans = page_dest.shape[0]
    block = 2 * tok + META
    rows = per_rank * QH * SPAN
    cosine, sine = (jnp.asarray(t) for t in tables(spans))
    ints = [pltpu.SMEM(x.shape, x.dtype) for x in (span_ids, lengths)]
    turns = [pltpu.VMEM(x.shape, x.dtype) for x in (cosine, sine)]
    packed = pl.pallas_call(
        functools.partial(prepare, spans),
        out_shape=pltpu.VMEM((block, HD), jnp.bfloat16),
        in_specs=[ANY] * 6,
        out_specs=VMEM,
        scratch_shapes=ints
        + [pltpu.VMEM(x.shape, x.dtype) for x in (keys, values)]
        + turns
        + [pltpu.SemaphoreType.DMA((6,))],
        compiler_params=LIMIT,
        name="prepare",
    )(*map(hbm, (span_ids, lengths, keys, values, cosine, sine)))

    def swap(x, distance):
        return lax.ppermute(x, "seq", [(i, i ^ distance) for i in range(ranks)])

    own = packed
    distance = ranks // 2
    while distance >= 16:
        own = jnp.concatenate([own, swap(own, distance)], axis=0)
        distance //= 2
    held = {"o": own}
    for name, source, distance in ROUTE:
        held[name] = swap(held[source], distance)

    state_shapes = tuple(pltpu.VMEM((rows, n), jnp.float32) for n in (HD, HD, HD))
    q_rot, *state = pl.pallas_call(
        functools.partial(early, spans),
        out_shape=(pltpu.VMEM((rows, HD), jnp.bfloat16), *state_shapes),
        in_specs=[ANY] * 5 + [VMEM],
        out_specs=(VMEM,) * 4,
        scratch_shapes=ints
        + [pltpu.VMEM(queries.shape, queries.dtype)]
        + turns
        + [pltpu.SemaphoreType.DMA((5,))],
        compiler_params=LIMIT,
        name="early",
    )(*map(hbm, (span_ids, lengths, queries, cosine, sine)), vmem(packed))

    first_page = (lax.axis_index("seq") * per_rank).astype(jnp.int32).reshape(1)
    pages_shape = jax.ShapeDtypeStruct((per_rank, SPAN, 2 * HD), jnp.bfloat16)

    def take(names, last, state, pages):
        pieces = [vmem(held[n]) for n in names]
        length = sum(p.shape[0] for p in pieces)
        units = length // block
        lane_groups = -(-units // HD)
        scratch = [
            pltpu.VMEM((units * 2 * tok, HD), jnp.bfloat16),
            pltpu.VMEM((per_rank, SPAN, 2 * HD), jnp.bfloat16),
            pltpu.VMEM((lane_groups, META, HD), jnp.int32),
            pltpu.SMEM((per_rank, units * per_rank + 4), jnp.int32),
            pltpu.SMEM((lane_groups, META, HD), jnp.int32),
            pltpu.SemaphoreType.DMA,
            pltpu.SemaphoreType.DMA((per_rank,)),
            pltpu.SemaphoreType.DMA((per_rank,)),
        ]
        if last:
            out_shape = (jax.ShapeDtypeStruct((tok, QH * HD), jnp.bfloat16), pages_shape)
            out_specs = (ANY, ANY)
            scratch = [
                *state_shapes,
                pltpu.VMEM((tok, QH * HD), jnp.bfloat16),
            ] + scratch
        else:
            out_shape = (*state_shapes, pages_shape)
            out_specs = (VMEM,) * 3 + (ANY,)
        inputs = [first_page, span_ids, lengths, page_dest, vmem(q_rot), *map(vmem, state), *pieces]
        in_specs = [SMEM] * 4 + [VMEM] * (4 + len(pieces))
        aliases = {}
        if last:
            aliases = {len(inputs): 1}
            inputs.append(pages)
            in_specs.append(ANY)
        return pl.pallas_call(
            functools.partial(absorb, per_rank, len(pieces), last),
            out_shape=out_shape,
            in_specs=in_specs,
            out_specs=out_specs,
            scratch_shapes=scratch,
            input_output_aliases=aliases,
            compiler_params=LIMIT,
            name="late" if last else "soon",
        )(*inputs)

    *state, pages = take(SOON, False, state, None)
    context, pages = take(LATE, True, state, pages)
    return context, pages


def solution(mesh):
    return jax.shard_map(
        functools.partial(on_device, mesh.shape["seq"]),
        mesh=mesh,
        in_specs=(
            P(("groups", "seq"), None),
            P(("groups", "seq"), None),
            P(("groups", "seq"), None),
            P(("groups", "seq")),
            P("groups"),
            P("groups"),
        ),
        out_specs=(P(("groups", "seq"), None), P(("groups", "seq"), None, None)),
        check_vma=False,
    )
```

profile of v0, /device:TPU:7, one launch (start us, length us, event | category | flops | bytes accessed | tf_op | source)
XLA Modules:
  0.0 38.7 jit_solution(421870951417841690)
XLA Ops:
  0.6 1.2 %prepare.1.refs_5_.rest_0_ = bf16[520,128]{1,0:T(8,128)(2,1)S(1)} custom-call(s32[2]{0:T(128)} %ids_ref.3, s32[8]{0:T(128)} %lengths_ref.3, bf16[256,128]{1,0:T(8,128)(2,1)} %refs_2_.2, bf16[256,128]{1,0:T(8,128)(2,1)} %refs_3_.2, f32[160,128]{1,0:T(8,128)} %constant.10.clone.refs_4_.refs_3_, f32[160,128]{1,0:T(8,128)} %constant.11.clone.refs_5_.refs_4_), custom_call_target="tpu_custom_call" | custom-call | tf_op jit(solution)/shard_map/prepare/pallas_call | solution.py:307
  1.8 2.4 %collective-permute-start.2 = (bf16[520,128]{1,0:T(8,128)(2,1)S(1)}, bf16[520,128]{1,0:T(8,128)(2,1)S(1)}, u32[]{:S(2)}, u32[]{:S(2)}) collective-permute-start(bf16[520,128]{1,0:T(8,128)(2,1)S(1)} %prepare.1.refs_5_.rest_0_), channel_id=1, source_target_pairs={{0,8},{1,9},{2,10},{3,11},{4,12},{5,13},{6,14},{7,15},{8,0},{9,1},... | collective-permute-start | bytes 399368 | tf_op jit(solution)/shard_map/ppermute | solution.py:321
  4.2 1.3 %collective-permute-start.1 = (bf16[520,128]{1,0:T(8,128)(2,1)S(1)}, bf16[520,128]{1,0:T(8,128)(2,1)S(1)}, u32[]{:S(2)}, u32[]{:S(2)}) collective-permute-start(bf16[520,128]{1,0:T(8,128)(2,1)S(1)} %prepare.1.refs_5_.rest_0_), channel_id=1, source_target_pairs={{0,4},{1,5},{2,6},{3,7},{4,0},{5,1},{6,2},{7,3},{8,12},{9,13},{10,... | collective-permute-start | bytes 399368 | tf_op jit(solution)/shard_map/ppermute | solution.py:321
  5.5 0.3 collective-permute-start
  5.7 1.5 %collective-permute-start.4 = (bf16[520,128]{1,0:T(8,128)(2,1)S(1)}, bf16[520,128]{1,0:T(8,128)(2,1)S(1)}, u32[]{:S(2)}, u32[]{:S(2)}) collective-permute-start(bf16[520,128]{1,0:T(8,128)(2,1)S(1)} %prepare.1.refs_5_.rest_0_), channel_id=1, source_target_pairs={{0,1},{1,0},{2,3},{3,2},{4,5},{5,4},{6,7},{7,6},{8,9},{9,8},{10,11... | collective-permute-start | bytes 399368 | tf_op jit(solution)/shard_map/ppermute | solution.py:321
  7.2 2.4 %collective-permute-done.2.rest_3_ = bf16[520,128]{1,0:T(8,128)(2,1)S(1)} collective-permute-done((bf16[520,128]{1,0:T(8,128)(2,1)S(1)}, bf16[520,128]{1,0:T(8,128)(2,1)S(1)}, u32[]{:S(2)}, u32[]{:S(2)}) %collective-permute-start.2) | collective-permute-done | bytes 133152 | tf_op jit(solution)/shard_map/ppermute | solution.py:321
  9.6 1.8 %collective-permute-start.3 = (bf16[520,128]{1,0:T(8,128)(2,1)S(1)}, bf16[520,128]{1,0:T(8,128)(2,1)}, u32[]{:S(2)}, u32[]{:S(2)}) collective-permute-start(bf16[520,128]{1,0:T(8,128)(2,1)S(1)} %collective-permute-done.2.rest_3_), channel_id=1, source_target_pairs={{0,4},{1,5},{2,6},{3,7},{4,0},{5,1},{6,2},{7,3},{8,12},{9,13},{10,... | collective-permute-start | bytes 399368 | tf_op jit(solution)/shard_map/ppermute | solution.py:321
  11.5 0.8 %collective-permute-start.7 = (bf16[520,128]{1,0:T(8,128)(2,1)S(1)}, bf16[520,128]{1,0:T(8,128)(2,1)S(1)}, u32[]{:S(2)}, u32[]{:S(2)}) collective-permute-start(bf16[520,128]{1,0:T(8,128)(2,1)S(1)} %collective-permute-done.2.rest_3_), channel_id=1, source_target_pairs={{0,1},{1,0},{2,3},{3,2},{4,5},{5,4},{6,7},{7,6},{8,9},{9,8},{10,11... | collective-permute-start | bytes 399368 | tf_op jit(solution)/shard_map/ppermute | solution.py:321
  12.2 0.0 collective-permute-start.6
  12.3 0.3 collective-permute-start.10
  12.6 1.2 %collective-permute-start.9 = (bf16[520,128]{1,0:T(8,128)(2,1)S(1)}, bf16[520,128]{1,0:T(8,128)(2,1)}, u32[]{:S(2)}, u32[]{:S(2)}) collective-permute-start(bf16[520,128]{1,0:T(8,128)(2,1)S(1)} %collective-permute-done.1.rest_2_), channel_id=1, source_target_pairs={{0,2},{1,3},{2,0},{3,1},{4,6},{5,7},{6,4},{7,5},{8,10},{9,11},{10,... | collective-permute-start | bytes 399368 | tf_op jit(solution)/shard_map/ppermute | solution.py:321
  13.8 0.2 collective-permute-done.3.rest_4_
  13.9 0.3 collective-permute-start.13
  14.2 0.7 %copy-done = bf16[520,128]{1,0:T(8,128)(2,1)} copy-done((bf16[520,128]{1,0:T(8,128)(2,1)}, bf16[520,128]{1,0:T(8,128)(2,1)S(1)}, u32[]{:S(2)}) %copy-start) | copy-done | bytes 133144
  14.9 3.1 %collective-permute-start.5 = (bf16[520,128]{1,0:T(8,128)(2,1)S(1)}, bf16[520,128]{1,0:T(8,128)(2,1)}, u32[]{:S(2)}, u32[]{:S(2)}) collective-permute-start(bf16[520,128]{1,0:T(8,128)(2,1)S(1)} %collective-permute-done.rest_1_), channel_id=1, source_target_pairs={{0,1},{1,0},{2,3},{3,2},{4,5},{5,4},{6,7},{7,6},{8,9},{9,8},{10,11... | collective-permute-start | bytes 399368 | tf_op jit(solution)/shard_map/ppermute | solution.py:321
  18.0 0.7 %copy-done.2 = bf16[520,128]{1,0:T(8,128)(2,1)} copy-done((bf16[520,128]{1,0:T(8,128)(2,1)}, bf16[520,128]{1,0:T(8,128)(2,1)S(1)}, u32[]{:S(2)}) %copy-start.2) | copy-done | bytes 133144
  18.6 0.7 %collective-permute-start.12 = (bf16[520,128]{1,0:T(8,128)(2,1)}, bf16[520,128]{1,0:T(8,128)(2,1)}, u32[]{:S(2)}, u32[]{:S(2)}) collective-permute-start(bf16[520,128]{1,0:T(8,128)(2,1)} %collective-permute-done.10.rest_2_), channel_id=1, source_target_pairs={{0,1},{1,0},{2,3},{3,2},{4,5},{5,4},{6,7},{7,6},{8,9},{9,8},{10,11... | collective-permute-start | bytes 399368 | tf_op jit(solution)/shard_map/ppermute | solution.py:321
  19.3 0.7 %collective-permute-done.9.rest_1_ = bf16[520,128]{1,0:T(8,128)(2,1)} collective-permute-done((bf16[520,128]{1,0:T(8,128)(2,1)S(1)}, bf16[520,128]{1,0:T(8,128)(2,1)}, u32[]{:S(2)}, u32[]{:S(2)}) %collective-permute-start.9) | collective-permute-done | bytes 133152 | tf_op jit(solution)/shard_map/ppermute | solution.py:321
  19.9 2.2 %collective-permute-start.11 = (bf16[520,128]{1,0:T(8,128)(2,1)}, bf16[520,128]{1,0:T(8,128)(2,1)}, u32[]{:S(2)}, u32[]{:S(2)}) collective-permute-start(bf16[520,128]{1,0:T(8,128)(2,1)} %collective-permute-done.9.rest_1_), channel_id=1, source_target_pairs={{0,1},{1,0},{2,3},{3,2},{4,5},{5,4},{6,7},{7,6},{8,9},{9,8},{10,11... | collective-permute-start | bytes 399368 | tf_op jit(solution)/shard_map/ppermute | solution.py:321
  22.1 0.7 %collective-permute-done.13.rest_5_ = bf16[520,128]{1,0:T(8,128)(2,1)} collective-permute-done((bf16[520,128]{1,0:T(8,128)(2,1)}, bf16[520,128]{1,0:T(8,128)(2,1)}, u32[]{:S(2)}, u32[]{:S(2)}) %collective-permute-start.13) | collective-permute-done | bytes 133152 | tf_op jit(solution)/shard_map/ppermute | solution.py:321
  22.8 1.3 %collective-permute-start.14 = (bf16[520,128]{1,0:T(8,128)(2,1)}, bf16[520,128]{1,0:T(8,128)(2,1)}, u32[]{:S(2)}, u32[]{:S(2)}) collective-permute-start(bf16[520,128]{1,0:T(8,128)(2,1)} %collective-permute-done.13.rest_5_), channel_id=1, source_target_pairs={{0,1},{1,0},{2,3},{3,2},{4,5},{5,4},{6,7},{7,6},{8,9},{9,8},{10,11... | collective-permute-start | bytes 399368 | tf_op jit(solution)/shard_map/ppermute | solution.py:321
  24.1 1.9 %early.1 = (bf16[1536,128]{1,0:T(8,128)(2,1)S(1)}, f32[1536,128]{1,0:T(8,128)S(1)}, f32[1536,128]{1,0:T(8,128)S(1)}, f32[1536,128]{1,0:T(8,128)S(1)}) custom-call(s32[2]{0:T(128)} %ids_ref.3, s32[8]{0:T(128)} %lengths_ref.3, bf16[256,768]{1,0:T(8,128)(2,1)} %refs_2_.3, f32[160,128]{1,0:T(8,128)} %constant.10.clone.refs_4_.refs_3_, ...), custom_call_target="tpu_custom_call" | custom-call | tf_op jit(solution)/shard_map/early/pallas_call | solution.py:333
  26.0 0.0 copy-start.4
  26.0 0.0 copy-start.5
  26.1 0.0 copy-start.6
  26.1 0.6 %copy-done.4 = s32[2]{0:T(128)S(1)} copy-done((s32[2]{0:T(128)S(1)}, s32[2]{0:T(128)}, u32[]{:S(2)}) %copy-start.4) | copy-done | bytes 32
  26.7 0.0 copy-done.5
  26.7 0.0 copy-done.6
  26.7 0.9 %copy-done.1 = bf16[520,128]{1,0:T(8,128)(2,1)S(1)} copy-done((bf16[520,128]{1,0:T(8,128)(2,1)S(1)}, bf16[520,128]{1,0:T(8,128)(2,1)}, u32[]{:S(2)}) %copy-start.1) | copy-done | bytes 133144
  27.6 0.9 %copy-done.3 = bf16[520,128]{1,0:T(8,128)(2,1)S(1)} copy-done((bf16[520,128]{1,0:T(8,128)(2,1)S(1)}, bf16[520,128]{1,0:T(8,128)(2,1)}, u32[]{:S(2)}) %copy-start.3) | copy-done | bytes 133144
  28.5 4.6 %soon.1 = (f32[1536,128]{1,0:T(8,128)S(1)}, f32[1536,128]{1,0:T(8,128)S(1)}, f32[1536,128]{1,0:T(8,128)S(1)}, bf16[2,128,256]{2,1,0:T(8,128)(2,1)}) custom-call(s32[1]{0:T(128)} %bitcast.first_page_ref, s32[2]{0:T(128)S(1)} %copy-done.4, s32[8]{0:T(128)S(1)} %copy-done.5, s32[32]{0:T(128)S(1)} %copy-done.6, bf16[1536,128]{1,0:T(8,128)(2,1)S(1)} %get-tuple-element.10.q_rot, ...), custom_call_target="tpu_custom_call" | custom-call | tf_op jit(solution)/shard_map/soon/pallas_call | solution.py:381
  33.1 5.6 %late.1 = (bf16[256,768]{1,0:T(8,128)(2,1)}, bf16[2,128,256]{2,1,0:T(8,128)(2,1)}) custom-call(s32[1]{0:T(128)} %bitcast.first_page_ref, s32[2]{0:T(128)S(1)} %copy-done.4, s32[8]{0:T(128)S(1)} %copy-done.5, s32[32]{0:T(128)S(1)} %copy-done.6, bf16[1536,128]{1,0:T(8,128)(2,1)S(1)} %get-tuple-element.10.q_rot, ...), custom_call_target="tpu_custom_call", output_to_operand_aliasing={{1}: (15, {})} | custom-call | tf_op jit(solution)/shard_map/late/pallas_call | solution.py:381
  (16 shorter events, 0.0 us)
Async XLA Ops:
  1.8 7.9 %collective-permute-start.2 = (bf16[520,128]{1,0:T(8,128)(2,1)S(1)}, bf16[520,128]{1,0:T(8,128)(2,1)S(1)}, u32[]{:S(2)}, u32[]{:S(2)}) collective-permute-start(bf16[520,128]{1,0:T(8,128)(2,1)S(1)} %prepare.1.refs_5_.rest_0_), channel_id=1, source_target_pairs={{0,8},{1,9},{2,10},{3,11},{4,12},{5,13},{6,14},{7,15},{8,0},{9,1},... | collective-permute-start | bytes 399368 | tf_op jit(solution)/shard_map/ppermute | solution.py:321
  4.2 8.1 %collective-permute-start.1 = (bf16[520,128]{1,0:T(8,128)(2,1)S(1)}, bf16[520,128]{1,0:T(8,128)(2,1)S(1)}, u32[]{:S(2)}, u32[]{:S(2)}) collective-permute-start(bf16[520,128]{1,0:T(8,128)(2,1)S(1)} %prepare.1.refs_5_.rest_0_), channel_id=1, source_target_pairs={{0,4},{1,5},{2,6},{3,7},{4,0},{5,1},{6,2},{7,3},{8,12},{9,13},{10,... | collective-permute-start | bytes 399368 | tf_op jit(solution)/shard_map/ppermute | solution.py:321
  5.5 6.8 %collective-permute-start = (bf16[520,128]{1,0:T(8,128)(2,1)S(1)}, bf16[520,128]{1,0:T(8,128)(2,1)S(1)}, u32[]{:S(2)}, u32[]{:S(2)}) collective-permute-start(bf16[520,128]{1,0:T(8,128)(2,1)S(1)} %prepare.1.refs_5_.rest_0_), channel_id=1, source_target_pairs={{0,2},{1,3},{2,0},{3,1},{4,6},{5,7},{6,4},{7,5},{8,10},{9,11},{10,... | collective-permute-start | bytes 399368 | tf_op jit(solution)/shard_map/ppermute | solution.py:321
  5.7 6.9 %collective-permute-start.4 = (bf16[520,128]{1,0:T(8,128)(2,1)S(1)}, bf16[520,128]{1,0:T(8,128)(2,1)S(1)}, u32[]{:S(2)}, u32[]{:S(2)}) collective-permute-start(bf16[520,128]{1,0:T(8,128)(2,1)S(1)} %prepare.1.refs_5_.rest_0_), channel_id=1, source_target_pairs={{0,1},{1,0},{2,3},{3,2},{4,5},{5,4},{6,7},{7,6},{8,9},{9,8},{10,11... | collective-permute-start | bytes 399368 | tf_op jit(solution)/shard_map/ppermute | solution.py:321
  9.6 4.3 %collective-permute-start.3 = (bf16[520,128]{1,0:T(8,128)(2,1)S(1)}, bf16[520,128]{1,0:T(8,128)(2,1)}, u32[]{:S(2)}, u32[]{:S(2)}) collective-permute-start(bf16[520,128]{1,0:T(8,128)(2,1)S(1)} %collective-permute-done.2.rest_3_), channel_id=1, source_target_pairs={{0,4},{1,5},{2,6},{3,7},{4,0},{5,1},{6,2},{7,3},{8,12},{9,13},{10,... | collective-permute-start | bytes 399368 | tf_op jit(solution)/shard_map/ppermute | solution.py:321
  11.5 2.7 %collective-permute-start.7 = (bf16[520,128]{1,0:T(8,128)(2,1)S(1)}, bf16[520,128]{1,0:T(8,128)(2,1)S(1)}, u32[]{:S(2)}, u32[]{:S(2)}) collective-permute-start(bf16[520,128]{1,0:T(8,128)(2,1)S(1)} %collective-permute-done.2.rest_3_), channel_id=1, source_target_pairs={{0,1},{1,0},{2,3},{3,2},{4,5},{5,4},{6,7},{7,6},{8,9},{9,8},{10,11... | collective-permute-start | bytes 399368 | tf_op jit(solution)/shard_map/ppermute | solution.py:321
  12.2 5.7 %collective-permute-start.6 = (bf16[520,128]{1,0:T(8,128)(2,1)S(1)}, bf16[520,128]{1,0:T(8,128)(2,1)S(1)}, u32[]{:S(2)}, u32[]{:S(2)}) collective-permute-start(bf16[520,128]{1,0:T(8,128)(2,1)S(1)} %collective-permute-done.1.rest_2_), channel_id=1, source_target_pairs={{0,1},{1,0},{2,3},{3,2},{4,5},{5,4},{6,7},{7,6},{8,9},{9,8},{10,11... | collective-permute-start | bytes 399368 | tf_op jit(solution)/shard_map/ppermute | solution.py:321
  12.3 6.4 %collective-permute-start.10 = (bf16[520,128]{1,0:T(8,128)(2,1)S(1)}, bf16[520,128]{1,0:T(8,128)(2,1)}, u32[]{:S(2)}, u32[]{:S(2)}) collective-permute-start(bf16[520,128]{1,0:T(8,128)(2,1)S(1)} %collective-permute-done.2.rest_3_), channel_id=1, source_target_pairs={{0,2},{1,3},{2,0},{3,1},{4,6},{5,7},{6,4},{7,5},{8,10},{9,11},{10,... | collective-permute-start | bytes 399368 | tf_op jit(solution)/shard_map/ppermute | solution.py:321
  12.6 7.4 %collective-permute-start.9 = (bf16[520,128]{1,0:T(8,128)(2,1)S(1)}, bf16[520,128]{1,0:T(8,128)(2,1)}, u32[]{:S(2)}, u32[]{:S(2)}) collective-permute-start(bf16[520,128]{1,0:T(8,128)(2,1)S(1)} %collective-permute-done.1.rest_2_), channel_id=1, source_target_pairs={{0,2},{1,3},{2,0},{3,1},{4,6},{5,7},{6,4},{7,5},{8,10},{9,11},{10,... | collective-permute-start | bytes 399368 | tf_op jit(solution)/shard_map/ppermute | solution.py:321
  13.9 8.8 %collective-permute-start.13 = (bf16[520,128]{1,0:T(8,128)(2,1)}, bf16[520,128]{1,0:T(8,128)(2,1)}, u32[]{:S(2)}, u32[]{:S(2)}) collective-permute-start(bf16[520,128]{1,0:T(8,128)(2,1)} %collective-permute-done.3.rest_4_), channel_id=1, source_target_pairs={{0,2},{1,3},{2,0},{3,1},{4,6},{5,7},{6,4},{7,5},{8,10},{9,11},{10,... | collective-permute-start | bytes 399368 | tf_op jit(solution)/shard_map/ppermute | solution.py:321
  14.2 0.7 %copy-start = (bf16[520,128]{1,0:T(8,128)(2,1)}, bf16[520,128]{1,0:T(8,128)(2,1)S(1)}, u32[]{:S(2)}) copy-start(bf16[520,128]{1,0:T(8,128)(2,1)S(1)} %collective-permute-done.7.rest_8_) | copy-start | bytes 399364
  14.9 11.2 %collective-permute-start.5 = (bf16[520,128]{1,0:T(8,128)(2,1)S(1)}, bf16[520,128]{1,0:T(8,128)(2,1)}, u32[]{:S(2)}, u32[]{:S(2)}) collective-permute-start(bf16[520,128]{1,0:T(8,128)(2,1)S(1)} %collective-permute-done.rest_1_), channel_id=1, source_target_pairs={{0,1},{1,0},{2,3},{3,2},{4,5},{5,4},{6,7},{7,6},{8,9},{9,8},{10,11... | collective-permute-start | bytes 399368 | tf_op jit(solution)/shard_map/ppermute | solution.py:321
  18.0 0.7 %copy-start.2 = (bf16[520,128]{1,0:T(8,128)(2,1)}, bf16[520,128]{1,0:T(8,128)(2,1)S(1)}, u32[]{:S(2)}) copy-start(bf16[520,128]{1,0:T(8,128)(2,1)S(1)} %collective-permute-done.6.rest_7_) | copy-start | bytes 399364
  18.6 14.5 %collective-permute-start.8 = (bf16[520,128]{1,0:T(8,128)(2,1)}, bf16[520,128]{1,0:T(8,128)(2,1)}, u32[]{:S(2)}, u32[]{:S(2)}) collective-permute-start(bf16[520,128]{1,0:T(8,128)(2,1)} %collective-permute-done.3.rest_4_), channel_id=1, source_target_pairs={{0,1},{1,0},{2,3},{3,2},{4,5},{5,4},{6,7},{7,6},{8,9},{9,8},{10,11... | collective-permute-start | bytes 399368 | tf_op jit(solution)/shard_map/ppermute | solution.py:321
  18.6 14.5 %collective-permute-start.12 = (bf16[520,128]{1,0:T(8,128)(2,1)}, bf16[520,128]{1,0:T(8,128)(2,1)}, u32[]{:S(2)}, u32[]{:S(2)}) collective-permute-start(bf16[520,128]{1,0:T(8,128)(2,1)} %collective-permute-done.10.rest_2_), channel_id=1, source_target_pairs={{0,1},{1,0},{2,3},{3,2},{4,5},{5,4},{6,7},{7,6},{8,9},{9,8},{10,11... | collective-permute-start | bytes 399368 | tf_op jit(solution)/shard_map/ppermute | solution.py:321
  19.9 13.2 %collective-permute-start.11 = (bf16[520,128]{1,0:T(8,128)(2,1)}, bf16[520,128]{1,0:T(8,128)(2,1)}, u32[]{:S(2)}, u32[]{:S(2)}) collective-permute-start(bf16[520,128]{1,0:T(8,128)(2,1)} %collective-permute-done.9.rest_1_), channel_id=1, source_target_pairs={{0,1},{1,0},{2,3},{3,2},{4,5},{5,4},{6,7},{7,6},{8,9},{9,8},{10,11... | collective-permute-start | bytes 399368 | tf_op jit(solution)/shard_map/ppermute | solution.py:321
  22.8 10.4 %collective-permute-start.14 = (bf16[520,128]{1,0:T(8,128)(2,1)}, bf16[520,128]{1,0:T(8,128)(2,1)}, u32[]{:S(2)}, u32[]{:S(2)}) collective-permute-start(bf16[520,128]{1,0:T(8,128)(2,1)} %collective-permute-done.13.rest_5_), channel_id=1, source_target_pairs={{0,1},{1,0},{2,3},{3,2},{4,5},{5,4},{6,7},{7,6},{8,9},{9,8},{10,11... | collective-permute-start | bytes 399368 | tf_op jit(solution)/shard_map/ppermute | solution.py:321
  26.0 0.7 %copy-start.4 = (s32[2]{0:T(128)S(1)}, s32[2]{0:T(128)}, u32[]{:S(2)}) copy-start(s32[2]{0:T(128)} %ids_ref.3) | copy-start | bytes 28
  26.0 0.7 %copy-start.5 = (s32[8]{0:T(128)S(1)}, s32[8]{0:T(128)}, u32[]{:S(2)}) copy-start(s32[8]{0:T(128)} %lengths_ref.3) | copy-start | bytes 100
  26.1 0.7 %copy-start.6 = (s32[32]{0:T(128)S(1)}, s32[32]{0:T(128)}, u32[]{:S(2)}) copy-start(s32[32]{0:T(128)} %dest_ref.3) | copy-start | bytes 388
  26.7 0.9 %copy-start.1 = (bf16[520,128]{1,0:T(8,128)(2,1)S(1)}, bf16[520,128]{1,0:T(8,128)(2,1)}, u32[]{:S(2)}) copy-start(bf16[520,128]{1,0:T(8,128)(2,1)} %copy-done) | copy-start | bytes 399364
  27.6 0.9 %copy-start.3 = (bf16[520,128]{1,0:T(8,128)(2,1)S(1)}, bf16[520,128]{1,0:T(8,128)(2,1)}, u32[]{:S(2)}) copy-start(bf16[520,128]{1,0:T(8,128)(2,1)} %copy-done.2) | copy-start | bytes 399364
where the time goes:
time: 39 us; the launch traced here: 38.7 us
  starting transfers between devices  17.1 us (44%)
  Pallas kernels  13.2 us (34%)
  waiting for transfers between devices  3.9 us (10%)
  local copies, waits for them, and re-layouts  3.79 us (10%)
  between operations  0.74 us (2%)
    ppermute x15, starting transfers between devices, swap(): return lax.ppermute(x, 'seq', [(i, i ^ distance) for i in range(ranks)])  17.1 us
    pallas_call x2, Pallas kernels, take(): pl.pallas_call(functools.partial(absorb, per_rank, len(pieces), last), ou...  10.2 us
    ppermute x15, waiting for transfers between devices, swap(): return lax.ppermute(x, 'seq', [(i, i ^ distance) for i in range(ranks)])  3.9 us
    unnamed x14, local copies, waits for them, and re-layouts  3.79 us
    pallas_call x1, Pallas kernels, plan(): pl.pallas_call(functools.partial(early, spans), out_shape=(pltpu.VMEM((ro...  1.92 us
    pallas_call x1, Pallas kernels, plan(): pl.pallas_call(functools.partial(prepare, spans), out_shape=pltpu.VMEM((b...  1.16 us
  transfers between devices with their start and end apart: 15, of which 4 were waited for; matrix products, arithmetic and copies ran while one was open for 0% of the time, Pallas kernels for 17%

commit v1 on v0

--- a/solution.py
+++ b/solution.py
@@ -113,9 +113,9 @@
 
 
 def early(spans, *refs):
+    own_ref = refs[5]
     q_rot, best, total, accum = refs[6:10]
     ids_ref, lengths_ref, queries_ref, cos_ref, sin_ref, sems = refs[10:]
-    own_ref = refs[5]
     for copy in fetch_all(list(zip(refs[:5], refs[10:15])), sems):
         copy.wait()
     tok = queries_ref.shape[0]
@@ -139,16 +139,17 @@
 
 
 def absorb(
-    per_rank, count, last, first_page_ref, ids_ref, lengths_ref, dest_ref, q_rot, best_in, total_in, accum_in, *rest
+    per_rank, count, last, ids_hbm, lengths_hbm, dest_hbm, q_rot, best_in, total_in, accum_in, *rest
 ):
     pieces, rest = rest[:count], rest[count:]
     if last:
-        _, context_ref, pages_ref, best, total, accum, rows_out = rest[:7]
+        _, best, total, accum, context_ref, pages_ref, rows_out = rest[:7]
         rest = rest[7:]
     else:
         best, total, accum, pages_ref = rest[:4]
         rest = rest[4:]
-    kv, page, ids_vmem, where, ids_smem, id_sem, page_sem, out_sem = rest
+    kv, page, ids_vmem, where, ids_smem, ids_ref, lengths_ref, dest_ref, in_sem, id_sem, page_sem, out_sem = rest
+    ints = fetch_all([(ids_hbm, ids_ref), (lengths_hbm, lengths_ref), (dest_hbm, dest_ref)], in_sem)
     tok = per_rank * SPAN
     rows = QH * SPAN
     block = 2 * tok + META
@@ -167,13 +168,11 @@
 
     for i, (piece, base) in enumerate(blocks):
         kv[2 * tok * i : 2 * tok * (i + 1), :] = piece[base : base + 2 * tok, :]
-    best[...] = best_in[...]
-    total[...] = total_in[...]
-    accum[...] = accum_in[...]
-
+    for copy in ints:
+        copy.wait()
     own_ids = [ids_ref[s] for s in range(per_rank)]
     starts = [history(span, lengths_ref) for span in own_ids]
-    first_page = first_page_ref[0]
+    first_page = lax.axis_index("seq") * per_rank
     fetch.wait()
 
     def note(i, found):
@@ -207,44 +206,66 @@
             page[p, :, HD:] = tile(found[per_rank + p] + tok)
             page_copy(p).start()
 
-    def step(s, places):
-        keys = jnp.concatenate([tile(p) for p in places], axis=0)
-        values = jnp.concatenate([tile(p + tok) for p in places], axis=0)
-        own = slice(s * rows, (s + 1) * rows)
-        scores = scores_of(q_rot[own, :], keys)
-        old = best[own, :]
-        top = jnp.maximum(old, jnp.max(scores, axis=1, keepdims=True))
-        factor = jnp.exp2((old - top) * SCALE)
-        weights = jnp.exp2((scores - jnp.tile(top, (1, len(places)))) * SCALE)
-        best[own, :] = top
-        total[own, :] = total[own, :] * factor + lanes(weights, jnp.add)
-        accum[own, :] = accum[own, :] * factor + jnp.dot(
-            weights.astype(jnp.bfloat16), values, preferred_element_type=jnp.float32
-        )
+    def step(at, size, *slots):
+        for s in slots:
+            places = [where[s, at[s] + i] for i in range(size)]
+            keys = jnp.concatenate([tile(p) for p in places], axis=0)
+            values = jnp.concatenate([tile(p + tok) for p in places], axis=0)
+            own = slice(s * rows, (s + 1) * rows)
+            scores = scores_of(q_rot[own, :], keys)
+            old = best[own, :]
+            top = jnp.maximum(old, jnp.max(scores, axis=1, keepdims=True))
+            factor = jnp.exp2((old - top) * SCALE)
+            weights = jnp.exp2((scores - jnp.tile(top, (1, size))) * SCALE)
+            best[own, :] = top
+            total[own, :] = total[own, :] * factor + lanes(weights, jnp.add)
+            accum[own, :] = accum[own, :] * factor + jnp.dot(
+                weights.astype(jnp.bfloat16), values, preferred_element_type=jnp.float32
+            )
+
+    def write(s):
+        own = slice(s * SPAN, (s + 1) * SPAN)
+        for h in range(QH):
+            part = slice(s * rows + h * SPAN, s * rows + (h + 1) * SPAN)
+            rows_out[own, h * HD : (h + 1) * HD] = (
+                accum[part, :] / jnp.sum(total[part, :], axis=1, keepdims=True)
+            ).astype(jnp.bfloat16)
+        return pltpu.make_async_copy(rows_out.at[own, :], context_ref.at[own, :], out_sem.at[s])
+
+    seen = found[:per_rank]
+    full = [n // LADDER[0] for n in seen]
+    shared = functools.reduce(jnp.minimum, full)
+    everyone = tuple(range(per_rank))
+
+    @pl.loop(0, shared)
+    def _(b):
+        step([LADDER[0] * b] * per_rank, LADDER[0], *everyone)
+
+    for s in everyone:
+
+        @pl.loop(shared, full[s])
+        def _(b):
+            step([LADDER[0] * b] * per_rank, LADDER[0], s)
+
+    for size in LADDER[1:]:
+        want = [n % (2 * size) >= size for n in seen]
+        at = [n // (2 * size) * (2 * size) for n in seen]
+        together = functools.reduce(jnp.logical_and, want)
+
+        @pl.when(together)
+        def _():
+            step(at, size, *everyone)
+
+        for s in everyone:
+
+            @pl.when(want[s] & jnp.logical_not(together))
+            def _():
+                step(at, size, s)
 
     outs = []
-    for s in range(per_rank):
-        seen = found[s]
-
-        @pl.loop(0, seen // LADDER[0])
-        def _(b):
-            step(s, [where[s, LADDER[0] * b + i] for i in range(LADDER[0])])
-
-        for size in LADDER[1:]:
-
-            @pl.when(seen % (2 * size) >= size)
-            def _():
-                base = seen // (2 * size) * (2 * size)
-                step(s, [where[s, base + i] for i in range(size)])
-
-        if last:
-            own = slice(s * SPAN, (s + 1) * SPAN)
-            for h in range(QH):
-                part = slice(s * rows + h * SPAN, s * rows + (h + 1) * SPAN)
-                rows_out[own, h * HD : (h + 1) * HD] = (
-                    accum[part, :] / jnp.sum(total[part, :], axis=1, keepdims=True)
-                ).astype(jnp.bfloat16)
-            outs.append(pltpu.make_async_copy(rows_out.at[own, :], context_ref.at[own, :], out_sem.at[s]))
+    if last:
+        for s in everyone:
+            outs.append(write(s))
             outs[-1].start()
 
     for copy in outs:
@@ -287,8 +308,8 @@
     ("cXA", "XA", 1),
     ("cXBA", "XBA", 1),
 )
-SOON = ("o", "X", "B", "A", "BA", "co", "cX", "cB", "cA")
-LATE = ("cBA", "XB", "XA", "cXB", "cXA", "XBA", "cXBA")
+SOON = ("o", "X", "B", "A", "BA", "co", "cX", "cB", "cA", "XB", "cBA")
+LATE = ("XA", "cXB", "cXA", "XBA", "cXBA")
 
 
 def on_device(ranks, queries, keys, values, span_ids, lengths, page_dest):
@@ -343,7 +364,6 @@
         name="early",
     )(*map(hbm, (span_ids, lengths, queries, cosine, sine)), vmem(packed))
 
-    first_page = (lax.axis_index("seq") * per_rank).astype(jnp.int32).reshape(1)
     pages_shape = jax.ShapeDtypeStruct((per_rank, SPAN, 2 * HD), jnp.bfloat16)
 
     def take(names, last, state, pages):
@@ -357,25 +377,25 @@
             pltpu.VMEM((lane_groups, META, HD), jnp.int32),
             pltpu.SMEM((per_rank, units * per_rank + 4), jnp.int32),
             pltpu.SMEM((lane_groups, META, HD), jnp.int32),
+            *[pltpu.SMEM(x.shape, x.dtype) for x in (span_ids, lengths, page_dest)],
+            pltpu.SemaphoreType.DMA((3,)),
             pltpu.SemaphoreType.DMA,
             pltpu.SemaphoreType.DMA((per_rank,)),
             pltpu.SemaphoreType.DMA((per_rank,)),
         ]
         if last:
-            out_shape = (jax.ShapeDtypeStruct((tok, QH * HD), jnp.bfloat16), pages_shape)
-            out_specs = (ANY, ANY)
-            scratch = [
-                *state_shapes,
-                pltpu.VMEM((tok, QH * HD), jnp.bfloat16),
-            ] + scratch
+            context_shape = jax.ShapeDtypeStruct((tok, QH * HD), jnp.bfloat16)
+            out_shape = (*state_shapes, context_shape, pages_shape)
+            out_specs = (VMEM,) * 3 + (ANY, ANY)
+            scratch = [pltpu.VMEM((tok, QH * HD), jnp.bfloat16)] + scratch
         else:
             out_shape = (*state_shapes, pages_shape)
             out_specs = (VMEM,) * 3 + (ANY,)
-        inputs = [first_page, span_ids, lengths, page_dest, vmem(q_rot), *map(vmem, state), *pieces]
-        in_specs = [SMEM] * 4 + [VMEM] * (4 + len(pieces))
-        aliases = {}
+        inputs = [*map(hbm, (span_ids, lengths, page_dest)), vmem(q_rot), *map(vmem, state), *pieces]
+        in_specs = [ANY] * 3 + [VMEM] * (4 + len(pieces))
+        aliases = {4: 0, 5: 1, 6: 2}
         if last:
-            aliases = {len(inputs): 1}
+            aliases[len(inputs)] = 4
             inputs.append(pages)
             in_specs.append(ANY)
         return pl.pallas_call(
@@ -390,7 +410,7 @@
         )(*inputs)
 
     *state, pages = take(SOON, False, state, None)
-    context, pages = take(LATE, True, state, pages)
+    *_, context, pages = take(LATE, True, state, pages)
     return context, pages
 
 

time: 39 us -> 34.4 us (0.88)
  local copies, waits for them, and re-layouts: 3.79 us -> 0 us
  Pallas kernels: 13.2 us -> 11.4 us
  waiting for transfers between devices: 3.9 us -> 5.63 us
  starting transfers between devices: 17.1 us -> 16.5 us
    unnamed x14 -> x0, local copies, waits for them, and re-layouts: 3.79 us -> none
    pallas_call x2, Pallas kernels: 10.2 us -> 8.28 us  [take(): pl.pallas_call(functools.partial(absorb, per_rank, len(pieces), last), ou...]
    ppermute x15, waiting for transfers between devices: 3.9 us -> 5.63 us  [swap(): return lax.ppermute(x, 'seq', [(i, i ^ distance) for i in range(ranks)])]
    ppermute x15, starting transfers between devices: 17.1 us -> 16.5 us  [swap(): return lax.ppermute(x, 'seq', [(i, i ^ distance) for i in range(ranks)])]
  transfers between devices with their start and end apart: 15 -> 15, of which waited for: 4 -> 4; matrix products, arithmetic and copies ran while one was open for 0% -> 0% of each run, Pallas kernels for 17% -> 21%
where the time goes in v1:
time: 34.4 us; the launch traced here: 34.2 us
  starting transfers between devices  16.5 us (48%)
  Pallas kernels  11.4 us (33%)
  waiting for transfers between devices  5.63 us (16%)
  between operations  0.71 us (2%)
    ppermute x15, starting transfers between devices, swap(): return lax.ppermute(x, 'seq', [(i, i ^ distance) for i in range(ranks)])  16.5 us
    pallas_call x2, Pallas kernels, take(): pl.pallas_call(functools.partial(absorb, per_rank, len(pieces), last), ou...  8.28 us
    ppermute x15, waiting for transfers between devices, swap(): return lax.ppermute(x, 'seq', [(i, i ^ distance) for i in range(ranks)])  5.63 us
    pallas_call x1, Pallas kernels, plan(): pl.pallas_call(functools.partial(early, spans), out_shape=(pltpu.VMEM((ro...  1.93 us
    pallas_call x1, Pallas kernels, plan(): pl.pallas_call(functools.partial(prepare, spans), out_shape=pltpu.VMEM((b...  1.16 us
  transfers between devices with their start and end apart: 15, of which 4 were waited for; matrix products, arithmetic and copies ran while one was open for 0% of the time, Pallas kernels for 21%

profile of v1, /device:TPU:7, one launch (start us, length us, event | category | flops | bytes accessed | tf_op | source)
XLA Modules:
  0.0 34.2 jit_solution(17803365808417314967)
XLA Ops:
  0.6 1.2 %prepare.1.refs_5_.rest_0_ = bf16[520,128]{1,0:T(8,128)(2,1)S(1)} custom-call(s32[2]{0:T(128)} %ids_hbm.3, s32[8]{0:T(128)} %lengths_hbm.3, bf16[256,128]{1,0:T(8,128)(2,1)} %refs_2_.2, bf16[256,128]{1,0:T(8,128)(2,1)} %refs_3_.2, f32[160,128]{1,0:T(8,128)} %constant.4.clone.refs_4_.refs_3_, f32[160,128]{1,0:T(8,128)} %constant.5.clone.refs_5_.refs_4_), custom_call_target="tpu_custom_call" | custom-call | tf_op jit(solution)/shard_map/prepare/pallas_call | solution.py:328
  1.8 2.4 %collective-permute-start.2 = (bf16[520,128]{1,0:T(8,128)(2,1)S(1)}, bf16[520,128]{1,0:T(8,128)(2,1)S(1)}, u32[]{:S(2)}, u32[]{:S(2)}) collective-permute-start(bf16[520,128]{1,0:T(8,128)(2,1)S(1)} %prepare.1.refs_5_.rest_0_), channel_id=1, source_target_pairs={{0,8},{1,9},{2,10},{3,11},{4,12},{5,13},{6,14},{7,15},{8,0},{9,1},... | collective-permute-start | bytes 399368 | tf_op jit(solution)/shard_map/ppermute | solution.py:342
  4.2 1.3 %collective-permute-start.1 = (bf16[520,128]{1,0:T(8,128)(2,1)S(1)}, bf16[520,128]{1,0:T(8,128)(2,1)S(1)}, u32[]{:S(2)}, u32[]{:S(2)}) collective-permute-start(bf16[520,128]{1,0:T(8,128)(2,1)S(1)} %prepare.1.refs_5_.rest_0_), channel_id=1, source_target_pairs={{0,4},{1,5},{2,6},{3,7},{4,0},{5,1},{6,2},{7,3},{8,12},{9,13},{10,... | collective-permute-start | bytes 399368 | tf_op jit(solution)/shard_map/ppermute | solution.py:342
  5.5 0.3 collective-permute-start
  5.7 1.5 %collective-permute-start.4 = (bf16[520,128]{1,0:T(8,128)(2,1)S(1)}, bf16[520,128]{1,0:T(8,128)(2,1)S(1)}, u32[]{:S(2)}, u32[]{:S(2)}) collective-permute-start(bf16[520,128]{1,0:T(8,128)(2,1)S(1)} %prepare.1.refs_5_.rest_0_), channel_id=1, source_target_pairs={{0,1},{1,0},{2,3},{3,2},{4,5},{5,4},{6,7},{7,6},{8,9},{9,8},{10,11... | collective-permute-start | bytes 399368 | tf_op jit(solution)/shard_map/ppermute | solution.py:342
  7.2 2.4 %collective-permute-done.2.rest_3_ = bf16[520,128]{1,0:T(8,128)(2,1)S(1)} collective-permute-done((bf16[520,128]{1,0:T(8,128)(2,1)S(1)}, bf16[520,128]{1,0:T(8,128)(2,1)S(1)}, u32[]{:S(2)}, u32[]{:S(2)}) %collective-permute-start.2) | collective-permute-done | bytes 133152 | tf_op jit(solution)/shard_map/ppermute | solution.py:342
  9.6 1.8 %collective-permute-start.3 = (bf16[520,128]{1,0:T(8,128)(2,1)S(1)}, bf16[520,128]{1,0:T(8,128)(2,1)S(1)}, u32[]{:S(2)}, u32[]{:S(2)}) collective-permute-start(bf16[520,128]{1,0:T(8,128)(2,1)S(1)} %collective-permute-done.2.rest_3_), channel_id=1, source_target_pairs={{0,4},{1,5},{2,6},{3,7},{4,0},{5,1},{6,2},{7,3},{8,12},{9,13},{10,... | collective-permute-start | bytes 399368 | tf_op jit(solution)/shard_map/ppermute | solution.py:342
  11.5 0.8 %collective-permute-start.7 = (bf16[520,128]{1,0:T(8,128)(2,1)S(1)}, bf16[520,128]{1,0:T(8,128)(2,1)S(1)}, u32[]{:S(2)}, u32[]{:S(2)}) collective-permute-start(bf16[520,128]{1,0:T(8,128)(2,1)S(1)} %collective-permute-done.2.rest_3_), channel_id=1, source_target_pairs={{0,1},{1,0},{2,3},{3,2},{4,5},{5,4},{6,7},{7,6},{8,9},{9,8},{10,11... | collective-permute-start | bytes 399368 | tf_op jit(solution)/shard_map/ppermute | solution.py:342
  12.2 0.0 collective-permute-done.1.rest_2_
  12.2 0.3 collective-permute-start.8
  12.5 0.0 collective-permute-done.rest_1_
  12.5 1.2 %collective-permute-start.10 = (bf16[520,128]{1,0:T(8,128)(2,1)S(1)}, bf16[520,128]{1,0:T(8,128)(2,1)S(1)}, u32[]{:S(2)}, u32[]{:S(2)}) collective-permute-start(bf16[520,128]{1,0:T(8,128)(2,1)S(1)} %collective-permute-done.2.rest_3_), channel_id=1, source_target_pairs={{0,2},{1,3},{2,0},{3,1},{4,6},{5,7},{6,4},{7,5},{8,10},{9,11},{10,... | collective-permute-start | bytes 399368 | tf_op jit(solution)/shard_map/ppermute | solution.py:342
  13.7 0.0 collective-permute-done.4.rest_5_
  13.7 0.6 %collective-permute-start.6 = (bf16[520,128]{1,0:T(8,128)(2,1)S(1)}, bf16[520,128]{1,0:T(8,128)(2,1)S(1)}, u32[]{:S(2)}, u32[]{:S(2)}) collective-permute-start(bf16[520,128]{1,0:T(8,128)(2,1)S(1)} %collective-permute-done.1.rest_2_), channel_id=1, source_target_pairs={{0,1},{1,0},{2,3},{3,2},{4,5},{5,4},{6,7},{7,6},{8,9},{9,8},{10,11... | collective-permute-start | bytes 399368 | tf_op jit(solution)/shard_map/ppermute | solution.py:342
  14.3 0.0 collective-permute-done.3.rest_4_
  14.3 0.3 collective-permute-start.13
  14.5 0.0 collective-permute-done.7.rest_8_
  14.5 2.7 %collective-permute-start.5 = (bf16[520,128]{1,0:T(8,128)(2,1)S(1)}, bf16[520,128]{1,0:T(8,128)(2,1)S(1)}, u32[]{:S(2)}, u32[]{:S(2)}) collective-permute-start(bf16[520,128]{1,0:T(8,128)(2,1)S(1)} %collective-permute-done.rest_1_), channel_id=1, source_target_pairs={{0,1},{1,0},{2,3},{3,2},{4,5},{5,4},{6,7},{7,6},{8,9},{9,8},{10,11... | collective-permute-start | bytes 399368 | tf_op jit(solution)/shard_map/ppermute | solution.py:342
  17.2 0.1 collective-permute-done.8.rest_9_
  17.3 1.3 %collective-permute-start.9 = (bf16[520,128]{1,0:T(8,128)(2,1)S(1)}, bf16[520,128]{1,0:T(8,128)(2,1)S(1)}, u32[]{:S(2)}, u32[]{:S(2)}) collective-permute-start(bf16[520,128]{1,0:T(8,128)(2,1)S(1)} %collective-permute-done.3.rest_4_), channel_id=1, source_target_pairs={{0,1},{1,0},{2,3},{3,2},{4,5},{5,4},{6,7},{7,6},{8,9},{9,8},{10,11... | collective-permute-start | bytes 399368 | tf_op jit(solution)/shard_map/ppermute | solution.py:342
  18.7 1.5 %collective-permute-done.10.rest_0_ = bf16[520,128]{1,0:T(8,128)(2,1)S(1)} collective-permute-done((bf16[520,128]{1,0:T(8,128)(2,1)S(1)}, bf16[520,128]{1,0:T(8,128)(2,1)S(1)}, u32[]{:S(2)}, u32[]{:S(2)}) %collective-permute-start.10) | collective-permute-done | bytes 133152 | tf_op jit(solution)/shard_map/ppermute | solution.py:342
  20.2 1.3 %collective-permute-start.12 = (bf16[520,128]{1,0:T(8,128)(2,1)S(1)}, bf16[520,128]{1,0:T(8,128)(2,1)S(1)}, u32[]{:S(2)}, u32[]{:S(2)}) collective-permute-start(bf16[520,128]{1,0:T(8,128)(2,1)S(1)} %collective-permute-done.10.rest_0_), channel_id=1, source_target_pairs={{0,1},{1,0},{2,3},{3,2},{4,5},{5,4},{6,7},{7,6},{8,9},{9,8},{10,11... | collective-permute-start | bytes 399368 | tf_op jit(solution)/shard_map/ppermute | solution.py:342
  21.5 0.0 collective-permute-done.6.rest_7_
  21.5 0.0 collective-permute-start.11
  21.5 1.5 %collective-permute-done.13.rest_3_ = bf16[520,128]{1,0:T(8,128)(2,1)S(1)} collective-permute-done((bf16[520,128]{1,0:T(8,128)(2,1)S(1)}, bf16[520,128]{1,0:T(8,128)(2,1)S(1)}, u32[]{:S(2)}, u32[]{:S(2)}) %collective-permute-start.13) | collective-permute-done | bytes 133152 | tf_op jit(solution)/shard_map/ppermute | solution.py:342
  23.0 0.9 %collective-permute-start.14 = (bf16[520,128]{1,0:T(8,128)(2,1)S(1)}, bf16[520,128]{1,0:T(8,128)(2,1)S(1)}, u32[]{:S(2)}, u32[]{:S(2)}) collective-permute-start(bf16[520,128]{1,0:T(8,128)(2,1)S(1)} %collective-permute-done.13.rest_3_), channel_id=1, source_target_pairs={{0,1},{1,0},{2,3},{3,2},{4,5},{5,4},{6,7},{7,6},{8,9},{9,8},{10,11... | collective-permute-start | bytes 399368 | tf_op jit(solution)/shard_map/ppermute | solution.py:342
  23.9 1.9 %early.1 = (bf16[1536,128]{1,0:T(8,128)(2,1)S(1)}, f32[1536,128]{1,0:T(8,128)S(1)}, f32[1536,128]{1,0:T(8,128)S(1)}, f32[1536,128]{1,0:T(8,128)S(1)}) custom-call(s32[2]{0:T(128)} %ids_hbm.3, s32[8]{0:T(128)} %lengths_hbm.3, bf16[256,768]{1,0:T(8,128)(2,1)} %refs_2_.3, f32[160,128]{1,0:T(8,128)} %constant.4.clone.refs_4_.refs_3_, ...), custom_call_target="tpu_custom_call" | custom-call | tf_op jit(solution)/shard_map/early/pallas_call | solution.py:354
  25.8 0.0 collective-permute-done.5.rest_6_
  25.9 5.1 %soon.1 = (f32[1536,128]{1,0:T(8,128)S(1)}, f32[1536,128]{1,0:T(8,128)S(1)}, f32[1536,128]{1,0:T(8,128)S(1)}, bf16[2,128,256]{2,1,0:T(8,128)(2,1)}) custom-call(s32[2]{0:T(128)} %ids_hbm.3, s32[8]{0:T(128)} %lengths_hbm.3, s32[32]{0:T(128)} %dest_hbm.3, ...), custom_call_target="tpu_custom_call", output_to_operand_aliasing={{0}: (4, {}), {1}: (5, {}), {2}: (6, {})} | custom-call | tf_op jit(solution)/shard_map/soon/pallas_call | solution.py:401
  31.0 0.0 collective-permute-done.12.rest_2_
  31.0 0.0 collective-permute-done.11.rest_1_
  31.0 3.2 %late.1 = (f32[1536,128]{1,0:T(8,128)S(1)}, f32[1536,128]{1,0:T(8,128)S(1)}, f32[1536,128]{1,0:T(8,128)S(1)}, bf16[256,768]{1,0:T(8,128)(2,1)}, bf16[2,128,256]{2,1,0:T(8,128)(2,1)}) custom-call(s32[2]{0:T(128)} %ids_hbm.3, s32[8]{0:T(128)} %lengths_hbm.3, s32[32]{0:T(128)} %dest_hbm.3, ...), custom_call_target="tpu_custom_call", output_to_operand_aliasing={{0}: (4, {}), {1}: (5, {}), {2}: (6, {}), {4}: (12, {})} | custom-call | tf_op jit(solution)/shard_map/late/pallas_call | solution.py:401
  (2 shorter events, 0.0 us)
Async XLA Ops:
  1.8 7.9 %collective-permute-start.2 = (bf16[520,128]{1,0:T(8,128)(2,1)S(1)}, bf16[520,128]{1,0:T(8,128)(2,1)S(1)}, u32[]{:S(2)}, u32[]{:S(2)}) collective-permute-start(bf16[520,128]{1,0:T(8,128)(2,1)S(1)} %prepare.1.refs_5_.rest_0_), channel_id=1, source_target_pairs={{0,8},{1,9},{2,10},{3,11},{4,12},{5,13},{6,14},{7,15},{8,0},{9,1},... | collective-permute-start | bytes 399368 | tf_op jit(solution)/shard_map/ppermute | solution.py:342
  4.2 8.1 %collective-permute-start.1 = (bf16[520,128]{1,0:T(8,128)(2,1)S(1)}, bf16[520,128]{1,0:T(8,128)(2,1)S(1)}, u32[]{:S(2)}, u32[]{:S(2)}) collective-permute-start(bf16[520,128]{1,0:T(8,128)(2,1)S(1)} %prepare.1.refs_5_.rest_0_), channel_id=1, source_target_pairs={{0,4},{1,5},{2,6},{3,7},{4,0},{5,1},{6,2},{7,3},{8,12},{9,13},{10,... | collective-permute-start | bytes 399368 | tf_op jit(solution)/shard_map/ppermute | solution.py:342
  5.5 7.0 %collective-permute-start = (bf16[520,128]{1,0:T(8,128)(2,1)S(1)}, bf16[520,128]{1,0:T(8,128)(2,1)S(1)}, u32[]{:S(2)}, u32[]{:S(2)}) collective-permute-start(bf16[520,128]{1,0:T(8,128)(2,1)S(1)} %prepare.1.refs_5_.rest_0_), channel_id=1, source_target_pairs={{0,2},{1,3},{2,0},{3,1},{4,6},{5,7},{6,4},{7,5},{8,10},{9,11},{10,... | collective-permute-start | bytes 399368 | tf_op jit(solution)/shard_map/ppermute | solution.py:342
  5.7 8.0 %collective-permute-start.4 = (bf16[520,128]{1,0:T(8,128)(2,1)S(1)}, bf16[520,128]{1,0:T(8,128)(2,1)S(1)}, u32[]{:S(2)}, u32[]{:S(2)}) collective-permute-start(bf16[520,128]{1,0:T(8,128)(2,1)S(1)} %prepare.1.refs_5_.rest_0_), channel_id=1, source_target_pairs={{0,1},{1,0},{2,3},{3,2},{4,5},{5,4},{6,7},{7,6},{8,9},{9,8},{10,11... | collective-permute-start | bytes 399368 | tf_op jit(solution)/shard_map/ppermute | solution.py:342
  9.6 4.6 %collective-permute-start.3 = (bf16[520,128]{1,0:T(8,128)(2,1)S(1)}, bf16[520,128]{1,0:T(8,128)(2,1)S(1)}, u32[]{:S(2)}, u32[]{:S(2)}) collective-permute-start(bf16[520,128]{1,0:T(8,128)(2,1)S(1)} %collective-permute-done.2.rest_3_), channel_id=1, source_target_pairs={{0,4},{1,5},{2,6},{3,7},{4,0},{5,1},{6,2},{7,3},{8,12},{9,13},{10,... | collective-permute-start | bytes 399368 | tf_op jit(solution)/shard_map/ppermute | solution.py:342
  11.5 3.1 %collective-permute-start.7 = (bf16[520,128]{1,0:T(8,128)(2,1)S(1)}, bf16[520,128]{1,0:T(8,128)(2,1)S(1)}, u32[]{:S(2)}, u32[]{:S(2)}) collective-permute-start(bf16[520,128]{1,0:T(8,128)(2,1)S(1)} %collective-permute-done.2.rest_3_), channel_id=1, source_target_pairs={{0,1},{1,0},{2,3},{3,2},{4,5},{5,4},{6,7},{7,6},{8,9},{9,8},{10,11... | collective-permute-start | bytes 399368 | tf_op jit(solution)/shard_map/ppermute | solution.py:342
  12.2 5.1 %collective-permute-start.8 = (bf16[520,128]{1,0:T(8,128)(2,1)S(1)}, bf16[520,128]{1,0:T(8,128)(2,1)S(1)}, u32[]{:S(2)}, u32[]{:S(2)}) collective-permute-start(bf16[520,128]{1,0:T(8,128)(2,1)S(1)} %collective-permute-done.1.rest_2_), channel_id=1, source_target_pairs={{0,2},{1,3},{2,0},{3,1},{4,6},{5,7},{6,4},{7,5},{8,10},{9,11},{10,... | collective-permute-start | bytes 399368 | tf_op jit(solution)/shard_map/ppermute | solution.py:342
  12.5 7.7 %collective-permute-start.10 = (bf16[520,128]{1,0:T(8,128)(2,1)S(1)}, bf16[520,128]{1,0:T(8,128)(2,1)S(1)}, u32[]{:S(2)}, u32[]{:S(2)}) collective-permute-start(bf16[520,128]{1,0:T(8,128)(2,1)S(1)} %collective-permute-done.2.rest_3_), channel_id=1, source_target_pairs={{0,2},{1,3},{2,0},{3,1},{4,6},{5,7},{6,4},{7,5},{8,10},{9,11},{10,... | collective-permute-start | bytes 399368 | tf_op jit(solution)/shard_map/ppermute | solution.py:342
  13.7 7.8 %collective-permute-start.6 = (bf16[520,128]{1,0:T(8,128)(2,1)S(1)}, bf16[520,128]{1,0:T(8,128)(2,1)S(1)}, u32[]{:S(2)}, u32[]{:S(2)}) collective-permute-start(bf16[520,128]{1,0:T(8,128)(2,1)S(1)} %collective-permute-done.1.rest_2_), channel_id=1, source_target_pairs={{0,1},{1,0},{2,3},{3,2},{4,5},{5,4},{6,7},{7,6},{8,9},{9,8},{10,11... | collective-permute-start | bytes 399368 | tf_op jit(solution)/shard_map/ppermute | solution.py:342
  14.3 8.8 %collective-permute-start.13 = (bf16[520,128]{1,0:T(8,128)(2,1)S(1)}, bf16[520,128]{1,0:T(8,128)(2,1)S(1)}, u32[]{:S(2)}, u32[]{:S(2)}) collective-permute-start(bf16[520,128]{1,0:T(8,128)(2,1)S(1)} %collective-permute-done.3.rest_4_), channel_id=1, source_target_pairs={{0,2},{1,3},{2,0},{3,1},{4,6},{5,7},{6,4},{7,5},{8,10},{9,11},{10,... | collective-permute-start | bytes 399368 | tf_op jit(solution)/shard_map/ppermute | solution.py:342
  14.5 11.3 %collective-permute-start.5 = (bf16[520,128]{1,0:T(8,128)(2,1)S(1)}, bf16[520,128]{1,0:T(8,128)(2,1)S(1)}, u32[]{:S(2)}, u32[]{:S(2)}) collective-permute-start(bf16[520,128]{1,0:T(8,128)(2,1)S(1)} %collective-permute-done.rest_1_), channel_id=1, source_target_pairs={{0,1},{1,0},{2,3},{3,2},{4,5},{5,4},{6,7},{7,6},{8,9},{9,8},{10,11... | collective-permute-start | bytes 399368 | tf_op jit(solution)/shard_map/ppermute | solution.py:342
  17.3 8.5 %collective-permute-start.9 = (bf16[520,128]{1,0:T(8,128)(2,1)S(1)}, bf16[520,128]{1,0:T(8,128)(2,1)S(1)}, u32[]{:S(2)}, u32[]{:S(2)}) collective-permute-start(bf16[520,128]{1,0:T(8,128)(2,1)S(1)} %collective-permute-done.3.rest_4_), channel_id=1, source_target_pairs={{0,1},{1,0},{2,3},{3,2},{4,5},{5,4},{6,7},{7,6},{8,9},{9,8},{10,11... | collective-permute-start | bytes 399368 | tf_op jit(solution)/shard_map/ppermute | solution.py:342
  20.2 10.8 %collective-permute-start.12 = (bf16[520,128]{1,0:T(8,128)(2,1)S(1)}, bf16[520,128]{1,0:T(8,128)(2,1)S(1)}, u32[]{:S(2)}, u32[]{:S(2)}) collective-permute-start(bf16[520,128]{1,0:T(8,128)(2,1)S(1)} %collective-permute-done.10.rest_0_), channel_id=1, source_target_pairs={{0,1},{1,0},{2,3},{3,2},{4,5},{5,4},{6,7},{7,6},{8,9},{9,8},{10,11... | collective-permute-start | bytes 399368 | tf_op jit(solution)/shard_map/ppermute | solution.py:342
  21.5 9.5 %collective-permute-start.11 = (bf16[520,128]{1,0:T(8,128)(2,1)S(1)}, bf16[520,128]{1,0:T(8,128)(2,1)S(1)}, u32[]{:S(2)}, u32[]{:S(2)}) collective-permute-start(bf16[520,128]{1,0:T(8,128)(2,1)S(1)} %collective-permute-done.8.rest_9_), channel_id=1, source_target_pairs={{0,1},{1,0},{2,3},{3,2},{4,5},{5,4},{6,7},{7,6},{8,9},{9,8},{10,11... | collective-permute-start | bytes 399368 | tf_op jit(solution)/shard_map/ppermute | solution.py:342
  23.0 7.9 %collective-permute-start.14 = (bf16[520,128]{1,0:T(8,128)(2,1)S(1)}, bf16[520,128]{1,0:T(8,128)(2,1)S(1)}, u32[]{:S(2)}, u32[]{:S(2)}) collective-permute-start(bf16[520,128]{1,0:T(8,128)(2,1)S(1)} %collective-permute-done.13.rest_3_), channel_id=1, source_target_pairs={{0,1},{1,0},{2,3},{3,2},{4,5},{5,4},{6,7},{7,6},{8,9},{9,8},{10,11... | collective-permute-start | bytes 399368 | tf_op jit(solution)/shard_map/ppermute | solution.py:342

commit v2 on v1

--- a/solution.py
+++ b/solution.py
@@ -113,19 +113,31 @@
 
 
 def early(spans, *refs):
-    own_ref = refs[5]
-    q_rot, best, total, accum = refs[6:10]
-    ids_ref, lengths_ref, queries_ref, cos_ref, sin_ref, sems = refs[10:]
-    for copy in fetch_all(list(zip(refs[:5], refs[10:15])), sems):
+    own_ref = refs[6]
+    info, q_rot, best, total, accum = refs[7:12]
+    ids_ref, lengths_ref, dest_ref, queries_ref, cos_ref, sin_ref, sems = refs[12:]
+    for copy in fetch_all(list(zip(refs[:6], refs[12:18])), sems):
         copy.wait()
     tok = queries_ref.shape[0]
+    per_rank = tok // SPAN
+    first_page = lax.axis_index("seq") * per_rank
+    for p in range(per_rank):
+
+        def sender(j, span):
+            return jnp.where(dest_ref[j] == first_page + p, j, span)
+
+        span = lax.fori_loop(0, spans, sender, jnp.int32(0), unroll=8)
+        info[2 * per_rank + p : 2 * per_rank + p + 1, :] = jnp.full((1, HD), span, jnp.int32)
     rows = QH * SPAN
     row = lax.broadcasted_iota(jnp.int32, (rows, SPAN), 0) % SPAN
     key = lax.broadcasted_iota(jnp.int32, (rows, SPAN), 1)
     causal = key <= row
     for s in range(tok // SPAN):
         span = ids_ref[s]
-        cosine, sine = turn(cos_ref, sin_ref, spans, span - history(span, lengths_ref))
+        start = history(span, lengths_ref)
+        info[s : s + 1, :] = jnp.full((1, HD), start, jnp.int32)
+        info[per_rank + s : per_rank + s + 1, :] = jnp.full((1, HD), span, jnp.int32)
+        cosine, sine = turn(cos_ref, sin_ref, spans, span - start)
         for h in range(QH):
             q_rot[s * rows + h * SPAN : s * rows + (h + 1) * SPAN, :] = rotary(
                 queries_ref[s * SPAN : (s + 1) * SPAN, h * HD : (h + 1) * HD], cosine, sine
@@ -139,7 +151,7 @@
 
 
 def absorb(
-    per_rank, count, last, ids_hbm, lengths_hbm, dest_hbm, q_rot, best_in, total_in, accum_in, *rest
+    per_rank, count, last, info, q_rot, best_in, total_in, accum_in, *rest
 ):
     pieces, rest = rest[:count], rest[count:]
     if last:
@@ -148,49 +160,45 @@
     else:
         best, total, accum, pages_ref = rest[:4]
         rest = rest[4:]
-    kv, page, ids_vmem, where, ids_smem, ids_ref, lengths_ref, dest_ref, in_sem, id_sem, page_sem, out_sem = rest
-    ints = fetch_all([(ids_hbm, ids_ref), (lengths_hbm, lengths_ref), (dest_hbm, dest_ref)], in_sem)
+    kv, page, where, page_sem, out_sem = rest
     tok = per_rank * SPAN
     rows = QH * SPAN
     block = 2 * tok + META
 
+    blocks = [(p, base) for p in pieces for base in range(0, p.shape[0], block)]
     lane = lax.broadcasted_iota(jnp.int32, (META, HD), 1)
-    blocks = [(p, base) for p in pieces for base in range(0, p.shape[0], block)]
-    for group in range(ids_vmem.shape[0]):
-        found = jnp.zeros((META, HD), jnp.float32)
-        for i in range(group * HD, min((group + 1) * HD, len(blocks))):
-            piece, base = blocks[i]
+    slot = lax.broadcasted_iota(jnp.int32, (META, HD), 0)
+    found = [jnp.int32(0)] * per_rank
+    pages = [jnp.int32(0)] * per_rank
+    group = 24 // per_rank
+    for first in range(0, len(blocks), group):
+        some = blocks[first : first + group]
+        numbers = jnp.full((META, HD), -1.0, jnp.float32)
+        for i, (piece, base) in enumerate(some):
             meta = piece[base + 2 * tok : base + block, :].astype(jnp.float32)
-            found = jnp.where(lane == i - group * HD, meta, found)
-        ids_vmem[group] = found.astype(jnp.int32)
-    fetch = pltpu.make_async_copy(ids_vmem, ids_smem, id_sem)
-    fetch.start()
+            numbers = jnp.where(lane == i, meta, numbers)
+        numbers = numbers.astype(jnp.int32)
+        valid = (slot < per_rank) & (lane < len(some))
+        weight = jnp.left_shift(1, jnp.where(valid, lane * per_rank + slot, 0)).astype(jnp.float32)
+        places = ((2 * (first + lane) * per_rank + slot) * SPAN + 1).astype(jnp.float32)
+
+        def row(i):
+            return info[i : i + 1, :]
+
+        def choose(mask, x):
+            return jnp.sum(jnp.where(mask & valid, x, 0.0)).astype(jnp.int32)
+
+        bits = [choose((numbers >= row(s)) & (numbers < row(per_rank + s)), weight) for s in range(per_rank)]
+        for p in range(per_rank):
+            pages[p] = pages[p] + choose(numbers == row(2 * per_rank + p), places)
+        for i in range(len(some)):
+            for j in range(per_rank):
+                for s in range(per_rank):
+                    where[s, found[s]] = (2 * (first + i) * per_rank + j) * SPAN
+                    found[s] = found[s] + (jnp.right_shift(bits[s], i * per_rank + j) & 1)
 
     for i, (piece, base) in enumerate(blocks):
         kv[2 * tok * i : 2 * tok * (i + 1), :] = piece[base : base + 2 * tok, :]
-    for copy in ints:
-        copy.wait()
-    own_ids = [ids_ref[s] for s in range(per_rank)]
-    starts = [history(span, lengths_ref) for span in own_ids]
-    first_page = lax.axis_index("seq") * per_rank
-    fetch.wait()
-
-    def note(i, found):
-        found = list(found)
-        for j in range(per_rank):
-            number = ids_smem[i // HD, j, i % HD]
-            place = (2 * i * per_rank + j) * SPAN
-            for s in range(per_rank):
-                where[s, found[s]] = place
-                seen = (number >= starts[s]) & (number < own_ids[s])
-                found[s] = found[s] + seen.astype(jnp.int32)
-            to = dest_ref[number] - first_page
-            for p in range(per_rank):
-                found[per_rank + p] = jnp.where(to == p, place, found[per_rank + p])
-        return tuple(found)
-
-    found = (jnp.int32(0),) * per_rank + (jnp.int32(-1),) * per_rank
-    found = lax.fori_loop(0, len(blocks), note, found, unroll=len(blocks) <= 16)
 
     def tile(place):
         return kv[pl.ds(pl.multiple_of(place, SPAN), SPAN), :]
@@ -200,10 +208,10 @@
 
     for p in range(per_rank):
 
-        @pl.when(found[per_rank + p] >= 0)
+        @pl.when(pages[p] > 0)
         def _():
-            page[p, :, :HD] = tile(found[per_rank + p])
-            page[p, :, HD:] = tile(found[per_rank + p] + tok)
+            page[p, :, :HD] = tile(pages[p] - 1)
+            page[p, :, HD:] = tile(pages[p] - 1 + tok)
             page_copy(p).start()
 
     def step(at, size, *slots):
@@ -232,7 +240,7 @@
             ).astype(jnp.bfloat16)
         return pltpu.make_async_copy(rows_out.at[own, :], context_ref.at[own, :], out_sem.at[s])
 
-    seen = found[:per_rank]
+    seen = found
     full = [n // LADDER[0] for n in seen]
     shared = functools.reduce(jnp.minimum, full)
     everyone = tuple(range(per_rank))
@@ -272,7 +280,7 @@
         copy.wait()
     for p in range(per_rank):
 
-        @pl.when(found[per_rank + p] >= 0)
+        @pl.when(pages[p] > 0)
         def _():
             page_copy(p).wait()
 
@@ -351,18 +359,22 @@
         held[name] = swap(held[source], distance)
 
     state_shapes = tuple(pltpu.VMEM((rows, n), jnp.float32) for n in (HD, HD, HD))
-    q_rot, *state = pl.pallas_call(
+    info, q_rot, *state = pl.pallas_call(
         functools.partial(early, spans),
-        out_shape=(pltpu.VMEM((rows, HD), jnp.bfloat16), *state_shapes),
-        in_specs=[ANY] * 5 + [VMEM],
-        out_specs=(VMEM,) * 4,
+        out_shape=(
+            pltpu.VMEM((-(-3 * per_rank // 8) * 8, HD), jnp.int32),
+            pltpu.VMEM((rows, HD), jnp.bfloat16),
+            *state_shapes,
+        ),
+        in_specs=[ANY] * 6 + [VMEM],
+        out_specs=(VMEM,) * 5,
         scratch_shapes=ints
-        + [pltpu.VMEM(queries.shape, queries.dtype)]
+        + [pltpu.SMEM(page_dest.shape, page_dest.dtype), pltpu.VMEM(queries.shape, queries.dtype)]
         + turns
-        + [pltpu.SemaphoreType.DMA((5,))],
+        + [pltpu.SemaphoreType.DMA((6,))],
         compiler_params=LIMIT,
         name="early",
-    )(*map(hbm, (span_ids, lengths, queries, cosine, sine)), vmem(packed))
+    )(*map(hbm, (span_ids, lengths, page_dest, queries, cosine, sine)), vmem(packed))
 
     pages_shape = jax.ShapeDtypeStruct((per_rank, SPAN, 2 * HD), jnp.bfloat16)
 
@@ -370,16 +382,10 @@
         pieces = [vmem(held[n]) for n in names]
         length = sum(p.shape[0] for p in pieces)
         units = length // block
-        lane_groups = -(-units // HD)
         scratch = [
             pltpu.VMEM((units * 2 * tok, HD), jnp.bfloat16),
             pltpu.VMEM((per_rank, SPAN, 2 * HD), jnp.bfloat16),
-            pltpu.VMEM((lane_groups, META, HD), jnp.int32),
             pltpu.SMEM((per_rank, units * per_rank + 4), jnp.int32),
-            pltpu.SMEM((lane_groups, META, HD), jnp.int32),
-            *[pltpu.SMEM(x.shape, x.dtype) for x in (span_ids, lengths, page_dest)],
-            pltpu.SemaphoreType.DMA((3,)),
-            pltpu.SemaphoreType.DMA,
             pltpu.SemaphoreType.DMA((per_rank,)),
             pltpu.SemaphoreType.DMA((per_rank,)),
         ]
@@ -391,9 +397,9 @@
         else:
             out_shape = (*state_shapes, pages_shape)
             out_specs = (VMEM,) * 3 + (ANY,)
-        inputs = [*map(hbm, (span_ids, lengths, page_dest)), vmem(q_rot), *map(vmem, state), *pieces]
-        in_specs = [ANY] * 3 + [VMEM] * (4 + len(pieces))
-        aliases = {4: 0, 5: 1, 6: 2}
+        inputs = [vmem(info), vmem(q_rot), *map(vmem, state), *pieces]
+        in_specs = [VMEM] * (5 + len(pieces))
+        aliases = {2: 0, 3: 1, 4: 2}
         if last:
             aliases[len(inputs)] = 4
             inputs.append(pages)

time: 34.4 us -> 33 us (0.959)
  Pallas kernels: 11.4 us -> 9.98 us
    pallas_call x2, Pallas kernels: 8.28 us -> 6.88 us  [take(): pl.pallas_call(functools.partial(absorb, per_rank, len(pieces), last), ou...]
  transfers between devices with their start and end apart: 15 -> 15, of which waited for: 4 -> 4; matrix products, arithmetic and copies ran while one was open for 0% -> 0% of each run, Pallas kernels for 21% -> 19%
where the time goes in v2:
time: 33 us; the launch traced here: 32.8 us
  starting transfers between devices  16.5 us (50%)
  Pallas kernels  9.98 us (30%)
  waiting for transfers between devices  5.63 us (17%)
  between operations  0.71 us (2%)
    ppermute x15, starting transfers between devices, swap(): return lax.ppermute(x, 'seq', [(i, i ^ distance) for i in range(ranks)])  16.5 us
    pallas_call x2, Pallas kernels, take(): pl.pallas_call(functools.partial(absorb, per_rank, len(pieces), last), ou...  6.88 us
    ppermute x15, waiting for transfers between devices, swap(): return lax.ppermute(x, 'seq', [(i, i ^ distance) for i in range(ranks)])  5.63 us
    pallas_call x1, Pallas kernels, plan(): pl.pallas_call(functools.partial(early, spans), out_shape=(pltpu.VMEM((-(...  1.94 us
    pallas_call x1, Pallas kernels, plan(): pl.pallas_call(functools.partial(prepare, spans), out_shape=pltpu.VMEM((b...  1.16 us
  transfers between devices with their start and end apart: 15, of which 4 were waited for; matrix products, arithmetic and copies ran while one was open for 0% of the time, Pallas kernels for 19%

profile of v2, /device:TPU:7, one launch (start us, length us, event | category | flops | bytes accessed | tf_op | source)
XLA Modules:
  0.0 32.8 jit_solution(14164559647039119226)
XLA Ops:
  0.6 1.2 %prepare.1.refs_6_.rest_0_ = bf16[520,128]{1,0:T(8,128)(2,1)S(1)} custom-call(s32[2]{0:T(128)} %refs_0_.3, s32[8]{0:T(128)} %refs_1_.3, bf16[256,128]{1,0:T(8,128)(2,1)} %refs_2_.2, bf16[256,128]{1,0:T(8,128)(2,1)} %refs_3_.2, f32[160,128]{1,0:T(8,128)} %constant.4.clone.refs_4_, f32[160,128]{1,0:T(8,128)} %constant.5.clone.refs_5_), custom_call_target="tpu_custom_call" | custom-call | tf_op jit(solution)/shard_map/prepare/pallas_call | solution.py:336
  1.8 2.4 %collective-permute-start.2 = (bf16[520,128]{1,0:T(8,128)(2,1)S(1)}, bf16[520,128]{1,0:T(8,128)(2,1)S(1)}, u32[]{:S(2)}, u32[]{:S(2)}) collective-permute-start(bf16[520,128]{1,0:T(8,128)(2,1)S(1)} %prepare.1.refs_6_.rest_0_), channel_id=1, source_target_pairs={{0,8},{1,9},{2,10},{3,11},{4,12},{5,13},{6,14},{7,15},{8,0},{9,1},... | collective-permute-start | bytes 399368 | tf_op jit(solution)/shard_map/ppermute | solution.py:350
  4.2 1.3 %collective-permute-start.1 = (bf16[520,128]{1,0:T(8,128)(2,1)S(1)}, bf16[520,128]{1,0:T(8,128)(2,1)S(1)}, u32[]{:S(2)}, u32[]{:S(2)}) collective-permute-start(bf16[520,128]{1,0:T(8,128)(2,1)S(1)} %prepare.1.refs_6_.rest_0_), channel_id=1, source_target_pairs={{0,4},{1,5},{2,6},{3,7},{4,0},{5,1},{6,2},{7,3},{8,12},{9,13},{10,... | collective-permute-start | bytes 399368 | tf_op jit(solution)/shard_map/ppermute | solution.py:350
  5.5 0.3 collective-permute-start
  5.7 1.5 %collective-permute-start.4 = (bf16[520,128]{1,0:T(8,128)(2,1)S(1)}, bf16[520,128]{1,0:T(8,128)(2,1)S(1)}, u32[]{:S(2)}, u32[]{:S(2)}) collective-permute-start(bf16[520,128]{1,0:T(8,128)(2,1)S(1)} %prepare.1.refs_6_.rest_0_), channel_id=1, source_target_pairs={{0,1},{1,0},{2,3},{3,2},{4,5},{5,4},{6,7},{7,6},{8,9},{9,8},{10,11... | collective-permute-start | bytes 399368 | tf_op jit(solution)/shard_map/ppermute | solution.py:350
  7.2 2.4 %collective-permute-done.2.rest_3_ = bf16[520,128]{1,0:T(8,128)(2,1)S(1)} collective-permute-done((bf16[520,128]{1,0:T(8,128)(2,1)S(1)}, bf16[520,128]{1,0:T(8,128)(2,1)S(1)}, u32[]{:S(2)}, u32[]{:S(2)}) %collective-permute-start.2) | collective-permute-done | bytes 133152 | tf_op jit(solution)/shard_map/ppermute | solution.py:350
  9.6 1.8 %collective-permute-start.3 = (bf16[520,128]{1,0:T(8,128)(2,1)S(1)}, bf16[520,128]{1,0:T(8,128)(2,1)S(1)}, u32[]{:S(2)}, u32[]{:S(2)}) collective-permute-start(bf16[520,128]{1,0:T(8,128)(2,1)S(1)} %collective-permute-done.2.rest_3_), channel_id=1, source_target_pairs={{0,4},{1,5},{2,6},{3,7},{4,0},{5,1},{6,2},{7,3},{8,12},{9,13},{10,... | collective-permute-start | bytes 399368 | tf_op jit(solution)/shard_map/ppermute | solution.py:350
  11.5 0.8 %collective-permute-start.7 = (bf16[520,128]{1,0:T(8,128)(2,1)S(1)}, bf16[520,128]{1,0:T(8,128)(2,1)S(1)}, u32[]{:S(2)}, u32[]{:S(2)}) collective-permute-start(bf16[520,128]{1,0:T(8,128)(2,1)S(1)} %collective-permute-done.2.rest_3_), channel_id=1, source_target_pairs={{0,1},{1,0},{2,3},{3,2},{4,5},{5,4},{6,7},{7,6},{8,9},{9,8},{10,11... | collective-permute-start | bytes 399368 | tf_op jit(solution)/shard_map/ppermute | solution.py:350
  12.2 0.0 collective-permute-done.1.rest_2_
  12.2 0.3 collective-permute-start.8
  12.5 0.0 collective-permute-done.rest_1_
  12.5 1.2 %collective-permute-start.10 = (bf16[520,128]{1,0:T(8,128)(2,1)S(1)}, bf16[520,128]{1,0:T(8,128)(2,1)S(1)}, u32[]{:S(2)}, u32[]{:S(2)}) collective-permute-start(bf16[520,128]{1,0:T(8,128)(2,1)S(1)} %collective-permute-done.2.rest_3_), channel_id=1, source_target_pairs={{0,2},{1,3},{2,0},{3,1},{4,6},{5,7},{6,4},{7,5},{8,10},{9,11},{10,... | collective-permute-start | bytes 399368 | tf_op jit(solution)/shard_map/ppermute | solution.py:350
  13.7 0.0 collective-permute-done.4.rest_5_
  13.7 0.6 %collective-permute-start.6 = (bf16[520,128]{1,0:T(8,128)(2,1)S(1)}, bf16[520,128]{1,0:T(8,128)(2,1)S(1)}, u32[]{:S(2)}, u32[]{:S(2)}) collective-permute-start(bf16[520,128]{1,0:T(8,128)(2,1)S(1)} %collective-permute-done.1.rest_2_), channel_id=1, source_target_pairs={{0,1},{1,0},{2,3},{3,2},{4,5},{5,4},{6,7},{7,6},{8,9},{9,8},{10,11... | collective-permute-start | bytes 399368 | tf_op jit(solution)/shard_map/ppermute | solution.py:350
  14.3 0.0 collective-permute-done.3.rest_4_
  14.3 0.3 collective-permute-start.13
  14.5 0.0 collective-permute-done.7.rest_8_
  14.5 2.7 %collective-permute-start.5 = (bf16[520,128]{1,0:T(8,128)(2,1)S(1)}, bf16[520,128]{1,0:T(8,128)(2,1)S(1)}, u32[]{:S(2)}, u32[]{:S(2)}) collective-permute-start(bf16[520,128]{1,0:T(8,128)(2,1)S(1)} %collective-permute-done.rest_1_), channel_id=1, source_target_pairs={{0,1},{1,0},{2,3},{3,2},{4,5},{5,4},{6,7},{7,6},{8,9},{9,8},{10,11... | collective-permute-start | bytes 399368 | tf_op jit(solution)/shard_map/ppermute | solution.py:350
  17.2 0.1 collective-permute-done.8.rest_9_
  17.3 1.3 %collective-permute-start.9 = (bf16[520,128]{1,0:T(8,128)(2,1)S(1)}, bf16[520,128]{1,0:T(8,128)(2,1)S(1)}, u32[]{:S(2)}, u32[]{:S(2)}) collective-permute-start(bf16[520,128]{1,0:T(8,128)(2,1)S(1)} %collective-permute-done.3.rest_4_), channel_id=1, source_target_pairs={{0,1},{1,0},{2,3},{3,2},{4,5},{5,4},{6,7},{7,6},{8,9},{9,8},{10,11... | collective-permute-start | bytes 399368 | tf_op jit(solution)/shard_map/ppermute | solution.py:350
  18.7 1.5 %collective-permute-done.10.rest_0_ = bf16[520,128]{1,0:T(8,128)(2,1)S(1)} collective-permute-done((bf16[520,128]{1,0:T(8,128)(2,1)S(1)}, bf16[520,128]{1,0:T(8,128)(2,1)S(1)}, u32[]{:S(2)}, u32[]{:S(2)}) %collective-permute-start.10) | collective-permute-done | bytes 133152 | tf_op jit(solution)/shard_map/ppermute | solution.py:350
  20.2 1.3 %collective-permute-start.12 = (bf16[520,128]{1,0:T(8,128)(2,1)S(1)}, bf16[520,128]{1,0:T(8,128)(2,1)S(1)}, u32[]{:S(2)}, u32[]{:S(2)}) collective-permute-start(bf16[520,128]{1,0:T(8,128)(2,1)S(1)} %collective-permute-done.10.rest_0_), channel_id=1, source_target_pairs={{0,1},{1,0},{2,3},{3,2},{4,5},{5,4},{6,7},{7,6},{8,9},{9,8},{10,11... | collective-permute-start | bytes 399368 | tf_op jit(solution)/shard_map/ppermute | solution.py:350
  21.5 0.0 collective-permute-done.6.rest_7_
  21.5 0.0 collective-permute-start.11
  21.5 1.5 %collective-permute-done.13.rest_3_ = bf16[520,128]{1,0:T(8,128)(2,1)S(1)} collective-permute-done((bf16[520,128]{1,0:T(8,128)(2,1)S(1)}, bf16[520,128]{1,0:T(8,128)(2,1)S(1)}, u32[]{:S(2)}, u32[]{:S(2)}) %collective-permute-start.13) | collective-permute-done | bytes 133152 | tf_op jit(solution)/shard_map/ppermute | solution.py:350
  23.0 0.9 %collective-permute-start.14 = (bf16[520,128]{1,0:T(8,128)(2,1)S(1)}, bf16[520,128]{1,0:T(8,128)(2,1)S(1)}, u32[]{:S(2)}, u32[]{:S(2)}) collective-permute-start(bf16[520,128]{1,0:T(8,128)(2,1)S(1)} %collective-permute-done.13.rest_3_), channel_id=1, source_target_pairs={{0,1},{1,0},{2,3},{3,2},{4,5},{5,4},{6,7},{7,6},{8,9},{9,8},{10,11... | collective-permute-start | bytes 399368 | tf_op jit(solution)/shard_map/ppermute | solution.py:350
  23.9 1.9 %early.1 = (s32[8,128]{1,0:T(8,128)S(1)}, bf16[1536,128]{1,0:T(8,128)(2,1)S(1)}, f32[1536,128]{1,0:T(8,128)S(1)}, f32[1536,128]{1,0:T(8,128)S(1)}, f32[1536,128]{1,0:T(8,128)S(1)}) custom-call(s32[2]{0:T(128)} %refs_0_.3, s32[8]{0:T(128)} %refs_1_.3, s32[32]{0:T(128)} %refs_2_.3, bf16[256,768]{1,0:T(8,128)(2,1)} %refs_3_.3, ...), custom_call_target="tpu_custom_call" | custom-call | tf_op jit(solution)/shard_map/early/pallas_call | solution.py:362
  25.9 0.0 collective-permute-done.9.rest_10_
  25.9 4.3 %soon.1 = (f32[1536,128]{1,0:T(8,128)S(1)}, f32[1536,128]{1,0:T(8,128)S(1)}, f32[1536,128]{1,0:T(8,128)S(1)}, bf16[2,128,256]{2,1,0:T(8,128)(2,1)}) custom-call(s32[8,128]{1,0:T(8,128)S(1)} %get-tuple-element.13.info, bf16[1536,128]{1,0:T(8,128)(2,1)S(1)} %get-tuple-element.14.q_rot, ...), custom_call_target="tpu_custom_call", output_to_operand_aliasing={{0}: (2, {}), {1}: (3, {}), {2}: (4, {})} | custom-call | tf_op jit(solution)/shard_map/soon/pallas_call | solution.py:407
  30.2 0.0 collective-permute-done.11.rest_1_
  30.2 0.0 collective-permute-done.14.rest_4_
  30.2 2.5 %late.1 = (f32[1536,128]{1,0:T(8,128)S(1)}, f32[1536,128]{1,0:T(8,128)S(1)}, f32[1536,128]{1,0:T(8,128)S(1)}, bf16[256,768]{1,0:T(8,128)(2,1)}, bf16[2,128,256]{2,1,0:T(8,128)(2,1)}) custom-call(s32[8,128]{1,0:T(8,128)S(1)} %get-tuple-element.13.info, ...), custom_call_target="tpu_custom_call", output_to_operand_aliasing={{0}: (2, {}), {1}: (3, {}), {2}: (4, {}), {4}: (10, {})} | custom-call | tf_op jit(solution)/shard_map/late/pallas_call | solution.py:407
  (2 shorter events, 0.0 us)
Async XLA Ops:
  1.8 7.9 %collective-permute-start.2 = (bf16[520,128]{1,0:T(8,128)(2,1)S(1)}, bf16[520,128]{1,0:T(8,128)(2,1)S(1)}, u32[]{:S(2)}, u32[]{:S(2)}) collective-permute-start(bf16[520,128]{1,0:T(8,128)(2,1)S(1)} %prepare.1.refs_6_.rest_0_), channel_id=1, source_target_pairs={{0,8},{1,9},{2,10},{3,11},{4,12},{5,13},{6,14},{7,15},{8,0},{9,1},... | collective-permute-start | bytes 399368 | tf_op jit(solution)/shard_map/ppermute | solution.py:350
  4.2 8.1 %collective-permute-start.1 = (bf16[520,128]{1,0:T(8,128)(2,1)S(1)}, bf16[520,128]{1,0:T(8,128)(2,1)S(1)}, u32[]{:S(2)}, u32[]{:S(2)}) collective-permute-start(bf16[520,128]{1,0:T(8,128)(2,1)S(1)} %prepare.1.refs_6_.rest_0_), channel_id=1, source_target_pairs={{0,4},{1,5},{2,6},{3,7},{4,0},{5,1},{6,2},{7,3},{8,12},{9,13},{10,... | collective-permute-start | bytes 399368 | tf_op jit(solution)/shard_map/ppermute | solution.py:350
  5.5 7.0 %collective-permute-start = (bf16[520,128]{1,0:T(8,128)(2,1)S(1)}, bf16[520,128]{1,0:T(8,128)(2,1)S(1)}, u32[]{:S(2)}, u32[]{:S(2)}) collective-permute-start(bf16[520,128]{1,0:T(8,128)(2,1)S(1)} %prepare.1.refs_6_.rest_0_), channel_id=1, source_target_pairs={{0,2},{1,3},{2,0},{3,1},{4,6},{5,7},{6,4},{7,5},{8,10},{9,11},{10,... | collective-permute-start | bytes 399368 | tf_op jit(solution)/shard_map/ppermute | solution.py:350
  5.7 8.0 %collective-permute-start.4 = (bf16[520,128]{1,0:T(8,128)(2,1)S(1)}, bf16[520,128]{1,0:T(8,128)(2,1)S(1)}, u32[]{:S(2)}, u32[]{:S(2)}) collective-permute-start(bf16[520,128]{1,0:T(8,128)(2,1)S(1)} %prepare.1.refs_6_.rest_0_), channel_id=1, source_target_pairs={{0,1},{1,0},{2,3},{3,2},{4,5},{5,4},{6,7},{7,6},{8,9},{9,8},{10,11... | collective-permute-start | bytes 399368 | tf_op jit(solution)/shard_map/ppermute | solution.py:350
  9.6 4.6 %collective-permute-start.3 = (bf16[520,128]{1,0:T(8,128)(2,1)S(1)}, bf16[520,128]{1,0:T(8,128)(2,1)S(1)}, u32[]{:S(2)}, u32[]{:S(2)}) collective-permute-start(bf16[520,128]{1,0:T(8,128)(2,1)S(1)} %collective-permute-done.2.rest_3_), channel_id=1, source_target_pairs={{0,4},{1,5},{2,6},{3,7},{4,0},{5,1},{6,2},{7,3},{8,12},{9,13},{10,... | collective-permute-start | bytes 399368 | tf_op jit(solution)/shard_map/ppermute | solution.py:350
  11.5 3.1 %collective-permute-start.7 = (bf16[520,128]{1,0:T(8,128)(2,1)S(1)}, bf16[520,128]{1,0:T(8,128)(2,1)S(1)}, u32[]{:S(2)}, u32[]{:S(2)}) collective-permute-start(bf16[520,128]{1,0:T(8,128)(2,1)S(1)} %collective-permute-done.2.rest_3_), channel_id=1, source_target_pairs={{0,1},{1,0},{2,3},{3,2},{4,5},{5,4},{6,7},{7,6},{8,9},{9,8},{10,11... | collective-permute-start | bytes 399368 | tf_op jit(solution)/shard_map/ppermute | solution.py:350
  12.2 5.1 %collective-permute-start.8 = (bf16[520,128]{1,0:T(8,128)(2,1)S(1)}, bf16[520,128]{1,0:T(8,128)(2,1)S(1)}, u32[]{:S(2)}, u32[]{:S(2)}) collective-permute-start(bf16[520,128]{1,0:T(8,128)(2,1)S(1)} %collective-permute-done.1.rest_2_), channel_id=1, source_target_pairs={{0,2},{1,3},{2,0},{3,1},{4,6},{5,7},{6,4},{7,5},{8,10},{9,11},{10,... | collective-permute-start | bytes 399368 | tf_op jit(solution)/shard_map/ppermute | solution.py:350
  12.5 7.7 %collective-permute-start.10 = (bf16[520,128]{1,0:T(8,128)(2,1)S(1)}, bf16[520,128]{1,0:T(8,128)(2,1)S(1)}, u32[]{:S(2)}, u32[]{:S(2)}) collective-permute-start(bf16[520,128]{1,0:T(8,128)(2,1)S(1)} %collective-permute-done.2.rest_3_), channel_id=1, source_target_pairs={{0,2},{1,3},{2,0},{3,1},{4,6},{5,7},{6,4},{7,5},{8,10},{9,11},{10,... | collective-permute-start | bytes 399368 | tf_op jit(solution)/shard_map/ppermute | solution.py:350
  13.7 7.8 %collective-permute-start.6 = (bf16[520,128]{1,0:T(8,128)(2,1)S(1)}, bf16[520,128]{1,0:T(8,128)(2,1)S(1)}, u32[]{:S(2)}, u32[]{:S(2)}) collective-permute-start(bf16[520,128]{1,0:T(8,128)(2,1)S(1)} %collective-permute-done.1.rest_2_), channel_id=1, source_target_pairs={{0,1},{1,0},{2,3},{3,2},{4,5},{5,4},{6,7},{7,6},{8,9},{9,8},{10,11... | collective-permute-start | bytes 399368 | tf_op jit(solution)/shard_map/ppermute | solution.py:350
  14.3 8.8 %collective-permute-start.13 = (bf16[520,128]{1,0:T(8,128)(2,1)S(1)}, bf16[520,128]{1,0:T(8,128)(2,1)S(1)}, u32[]{:S(2)}, u32[]{:S(2)}) collective-permute-start(bf16[520,128]{1,0:T(8,128)(2,1)S(1)} %collective-permute-done.3.rest_4_), channel_id=1, source_target_pairs={{0,2},{1,3},{2,0},{3,1},{4,6},{5,7},{6,4},{7,5},{8,10},{9,11},{10,... | collective-permute-start | bytes 399368 | tf_op jit(solution)/shard_map/ppermute | solution.py:350
  14.5 11.3 %collective-permute-start.5 = (bf16[520,128]{1,0:T(8,128)(2,1)S(1)}, bf16[520,128]{1,0:T(8,128)(2,1)S(1)}, u32[]{:S(2)}, u32[]{:S(2)}) collective-permute-start(bf16[520,128]{1,0:T(8,128)(2,1)S(1)} %collective-permute-done.rest_1_), channel_id=1, source_target_pairs={{0,1},{1,0},{2,3},{3,2},{4,5},{5,4},{6,7},{7,6},{8,9},{9,8},{10,11... | collective-permute-start | bytes 399368 | tf_op jit(solution)/shard_map/ppermute | solution.py:350
  17.3 8.5 %collective-permute-start.9 = (bf16[520,128]{1,0:T(8,128)(2,1)S(1)}, bf16[520,128]{1,0:T(8,128)(2,1)S(1)}, u32[]{:S(2)}, u32[]{:S(2)}) collective-permute-start(bf16[520,128]{1,0:T(8,128)(2,1)S(1)} %collective-permute-done.3.rest_4_), channel_id=1, source_target_pairs={{0,1},{1,0},{2,3},{3,2},{4,5},{5,4},{6,7},{7,6},{8,9},{9,8},{10,11... | collective-permute-start | bytes 399368 | tf_op jit(solution)/shard_map/ppermute | solution.py:350
  20.2 10.0 %collective-permute-start.12 = (bf16[520,128]{1,0:T(8,128)(2,1)S(1)}, bf16[520,128]{1,0:T(8,128)(2,1)S(1)}, u32[]{:S(2)}, u32[]{:S(2)}) collective-permute-start(bf16[520,128]{1,0:T(8,128)(2,1)S(1)} %collective-permute-done.10.rest_0_), channel_id=1, source_target_pairs={{0,1},{1,0},{2,3},{3,2},{4,5},{5,4},{6,7},{7,6},{8,9},{9,8},{10,11... | collective-permute-start | bytes 399368 | tf_op jit(solution)/shard_map/ppermute | solution.py:350
  21.5 8.7 %collective-permute-start.11 = (bf16[520,128]{1,0:T(8,128)(2,1)S(1)}, bf16[520,128]{1,0:T(8,128)(2,1)S(1)}, u32[]{:S(2)}, u32[]{:S(2)}) collective-permute-start(bf16[520,128]{1,0:T(8,128)(2,1)S(1)} %collective-permute-done.8.rest_9_), channel_id=1, source_target_pairs={{0,1},{1,0},{2,3},{3,2},{4,5},{5,4},{6,7},{7,6},{8,9},{9,8},{10,11... | collective-permute-start | bytes 399368 | tf_op jit(solution)/shard_map/ppermute | solution.py:350
  23.0 7.2 %collective-permute-start.14 = (bf16[520,128]{1,0:T(8,128)(2,1)S(1)}, bf16[520,128]{1,0:T(8,128)(2,1)S(1)}, u32[]{:S(2)}, u32[]{:S(2)}) collective-permute-start(bf16[520,128]{1,0:T(8,128)(2,1)S(1)} %collective-permute-done.13.rest_3_), channel_id=1, source_target_pairs={{0,1},{1,0},{2,3},{3,2},{4,5},{5,4},{6,7},{7,6},{8,9},{9,8},{10,11... | collective-permute-start | bytes 399368 | tf_op jit(solution)/shard_map/ppermute | solution.py:350

commit v3 on v2

--- a/solution.py
+++ b/solution.py
@@ -76,7 +76,7 @@
     out_ref[2 * rows :, :] = meta.astype(jnp.bfloat16)
 
 
-LADDER = (4, 2, 1)
+LADDER = 4
 
 
 def lanes(x, combine):
@@ -151,12 +151,13 @@
 
 
 def absorb(
-    per_rank, count, last, info, q_rot, best_in, total_in, accum_in, *rest
+    per_rank, count, fresh, last, info, q_rot, best_in, total_in, accum_in, *rest
 ):
     pieces, rest = rest[:count], rest[count:]
+    rest = rest[0 if fresh else 1 :]
     if last:
-        _, best, total, accum, context_ref, pages_ref, rows_out = rest[:7]
-        rest = rest[7:]
+        best, total, accum, context_ref, pages_ref, rows_out = rest[:6]
+        rest = rest[6:]
     else:
         best, total, accum, pages_ref = rest[:4]
         rest = rest[4:]
@@ -215,21 +216,33 @@
             page_copy(p).start()
 
     def step(at, size, *slots):
-        for s in slots:
-            places = [where[s, at[s] + i] for i in range(size)]
-            keys = jnp.concatenate([tile(p) for p in places], axis=0)
-            values = jnp.concatenate([tile(p + tok) for p in places], axis=0)
-            own = slice(s * rows, (s + 1) * rows)
-            scores = scores_of(q_rot[own, :], keys)
-            old = best[own, :]
-            top = jnp.maximum(old, jnp.max(scores, axis=1, keepdims=True))
-            factor = jnp.exp2((old - top) * SCALE)
-            weights = jnp.exp2((scores - jnp.tile(top, (1, size))) * SCALE)
-            best[own, :] = top
-            total[own, :] = total[own, :] * factor + lanes(weights, jnp.add)
-            accum[own, :] = accum[own, :] * factor + jnp.dot(
-                weights.astype(jnp.bfloat16), values, preferred_element_type=jnp.float32
-            )
+        places = [[where[s, at[s] + i] for i in range(size)] for s in slots]
+        own = slice(slots[0] * rows, (slots[-1] + 1) * rows)
+        scores = jnp.concatenate(
+            [
+                scores_of(q_rot[s * rows : (s + 1) * rows, :], jnp.concatenate([tile(p) for p in some], axis=0))
+                for s, some in zip(slots, places)
+            ],
+            axis=0,
+        )
+        old = best[own, :]
+        top = jnp.maximum(old, jnp.max(scores, axis=1, keepdims=True))
+        factor = jnp.exp2((old - top) * SCALE)
+        weights = jnp.exp2((scores - jnp.tile(top, (1, size))) * SCALE)
+        best[own, :] = top
+        total[own, :] = total[own, :] * factor + lanes(weights, jnp.add)
+        weights = weights.astype(jnp.bfloat16)
+        accum[own, :] = accum[own, :] * factor + jnp.concatenate(
+            [
+                jnp.dot(
+                    weights[i * rows : (i + 1) * rows, :],
+                    jnp.concatenate([tile(p + tok) for p in some], axis=0),
+                    preferred_element_type=jnp.float32,
+                )
+                for i, some in enumerate(places)
+            ],
+            axis=0,
+        )
 
     def write(s):
         own = slice(s * SPAN, (s + 1) * SPAN)
@@ -241,23 +254,23 @@
         return pltpu.make_async_copy(rows_out.at[own, :], context_ref.at[own, :], out_sem.at[s])
 
     seen = found
-    full = [n // LADDER[0] for n in seen]
+    full = [n // LADDER for n in seen]
     shared = functools.reduce(jnp.minimum, full)
     everyone = tuple(range(per_rank))
 
     @pl.loop(0, shared)
     def _(b):
-        step([LADDER[0] * b] * per_rank, LADDER[0], *everyone)
+        step([LADDER * b] * per_rank, LADDER, *everyone)
 
     for s in everyone:
 
         @pl.loop(shared, full[s])
         def _(b):
-            step([LADDER[0] * b] * per_rank, LADDER[0], s)
-
-    for size in LADDER[1:]:
-        want = [n % (2 * size) >= size for n in seen]
-        at = [n // (2 * size) * (2 * size) for n in seen]
+            step([LADDER * b] * per_rank, LADDER, s)
+
+    at = [LADDER * n for n in full]
+    for size in range(LADDER - 1, 0, -1):
+        want = [n % LADDER == size for n in seen]
         together = functools.reduce(jnp.logical_and, want)
 
         @pl.when(together)
@@ -300,24 +313,25 @@
 
 
 ROUTE = (
-    ("A", "o", 8),
-    ("B", "o", 4),
-    ("X", "o", 2),
-    ("co", "o", 1),
-    ("BA", "A", 4),
-    ("XB", "B", 2),
-    ("XA", "A", 2),
-    ("cX", "X", 1),
-    ("cA", "A", 1),
-    ("cB", "B", 1),
-    ("XBA", "BA", 2),
-    ("cBA", "BA", 1),
-    ("cXB", "XB", 1),
-    ("cXA", "XA", 1),
-    ("cXBA", "XBA", 1),
+    ("v1", "o", 4, 8),
+    ("v2", "o", 8, 2),
+    ("v3", "o", 2, 4),
+    ("co", "o", 1, 1),
+    ("v4", "v1", 2, 2),
+    ("v5", "v1", 8, 4),
+    ("v6", "v2", 2, 4),
+    ("cv3", "v3", 1, 1),
+    ("cv1", "v1", 1, 1),
+    ("cv2", "v2", 1, 1),
+    ("v7", "v4", 8, 4),
+    ("cv4", "v4", 1, 1),
+    ("cv5", "v5", 1, 1),
+    ("cv6", "v6", 1, 1),
+    ("cv7", "v7", 1, 1),
 )
-SOON = ("o", "X", "B", "A", "BA", "co", "cX", "cB", "cA", "XB", "cBA")
-LATE = ("XA", "cXB", "cXA", "XBA", "cXBA")
+SOON = ("o", "v1", "v2", "v3", "co", "cv1", "cv2", "cv3", "v4", "cv4", "v5")
+MID = ("v6", "cv5", "v7")
+LATE = ("cv6", "cv7")
 
 
 def on_device(ranks, queries, keys, values, span_ids, lengths, page_dest):
@@ -346,17 +360,17 @@
         name="prepare",
     )(*map(hbm, (span_ids, lengths, keys, values, cosine, sine)))
 
-    def swap(x, distance):
-        return lax.ppermute(x, "seq", [(i, i ^ distance) for i in range(ranks)])
+    def swap(x, even, odd):
+        return lax.ppermute(x, "seq", [(i, i ^ (odd if i % 2 else even)) for i in range(ranks)])
 
     own = packed
     distance = ranks // 2
     while distance >= 16:
-        own = jnp.concatenate([own, swap(own, distance)], axis=0)
+        own = jnp.concatenate([own, swap(own, distance, distance)], axis=0)
         distance //= 2
     held = {"o": own}
-    for name, source, distance in ROUTE:
-        held[name] = swap(held[source], distance)
+    for name, source, even, odd in ROUTE:
+        held[name] = swap(held[source], even, odd)
 
     state_shapes = tuple(pltpu.VMEM((rows, n), jnp.float32) for n in (HD, HD, HD))
     info, q_rot, *state = pl.pallas_call(
@@ -378,7 +392,7 @@
 
     pages_shape = jax.ShapeDtypeStruct((per_rank, SPAN, 2 * HD), jnp.bfloat16)
 
-    def take(names, last, state, pages):
+    def take(names, state, pages, last=False):
         pieces = [vmem(held[n]) for n in names]
         length = sum(p.shape[0] for p in pieces)
         units = length // block
@@ -400,23 +414,23 @@
         inputs = [vmem(info), vmem(q_rot), *map(vmem, state), *pieces]
         in_specs = [VMEM] * (5 + len(pieces))
         aliases = {2: 0, 3: 1, 4: 2}
-        if last:
-            aliases[len(inputs)] = 4
+        if pages is not None:
+            aliases[len(inputs)] = len(out_shape) - 1
             inputs.append(pages)
             in_specs.append(ANY)
         return pl.pallas_call(
-            functools.partial(absorb, per_rank, len(pieces), last),
+            functools.partial(absorb, per_rank, len(pieces), pages is None, last),
             out_shape=out_shape,
             in_specs=in_specs,
             out_specs=out_specs,
             scratch_shapes=scratch,
             input_output_aliases=aliases,
             compiler_params=LIMIT,
-            name="late" if last else "soon",
         )(*inputs)
 
-    *state, pages = take(SOON, False, state, None)
-    *_, context, pages = take(LATE, True, state, pages)
+    *state, pages = take(SOON, state, None)
+    *state, pages = take(MID, state, pages)
+    *_, context, pages = take(LATE, state, pages, last=True)
     return context, pages
 
 

time: 33 us -> 32.7 us (level)
  waiting for transfers between devices: 5.63 us -> 4.38 us
  starting transfers between devices: 16.5 us -> 17.2 us
    ppermute x15, waiting for transfers between devices: 5.63 us -> 4.38 us  [swap(): lax.ppermute(x, 'seq', [(i, i ^ (odd if i % 2 else even)) for i in range(...]
    ppermute x15, starting transfers between devices: 16.5 us -> 17.2 us  [swap(): lax.ppermute(x, 'seq', [(i, i ^ (odd if i % 2 else even)) for i in range(...]
    pallas_call x2 -> x3, Pallas kernels: 6.88 us -> 7 us  [take(): pl.pallas_call(functools.partial(absorb, per_rank, len(pieces), pages is...]
  transfers between devices with their start and end apart: 15 -> 15, of which waited for: 4 -> 3; matrix products, arithmetic and copies ran while one was open for 0% -> 0% of each run, Pallas kernels for 19% -> 22%
where the time goes in v3:
time: 32.7 us; the launch traced here: 32.5 us
  starting transfers between devices  17.2 us (53%)
  Pallas kernels  10.1 us (31%)
  waiting for transfers between devices  4.38 us (13%)
  between operations  0.87 us (3%)
    ppermute x15, starting transfers between devices, swap(): lax.ppermute(x, 'seq', [(i, i ^ (odd if i % 2 else even)) for i in range(...  17.2 us
    pallas_call x3, Pallas kernels, take(): pl.pallas_call(functools.partial(absorb, per_rank, len(pieces), pages is...  7 us
    ppermute x15, waiting for transfers between devices, swap(): lax.ppermute(x, 'seq', [(i, i ^ (odd if i % 2 else even)) for i in range(...  4.38 us
    pallas_call x1, Pallas kernels, plan(): pl.pallas_call(functools.partial(early, spans), out_shape=(pltpu.VMEM((-(...  1.94 us
    pallas_call x1, Pallas kernels, plan(): pl.pallas_call(functools.partial(prepare, spans), out_shape=pltpu.VMEM((b...  1.16 us
  transfers between devices with their start and end apart: 15, of which 3 were waited for; matrix products, arithmetic and copies ran while one was open for 0% of the time, Pallas kernels for 22%

profile of v3, /device:TPU:7, one launch (start us, length us, event | category | flops | bytes accessed | tf_op | source)
XLA Modules:
  0.0 32.5 jit_solution(12578601888043417910)
XLA Ops:
  0.6 1.2 %prepare.1.refs_6_.rest_0_ = bf16[520,128]{1,0:T(8,128)(2,1)S(1)} custom-call(s32[2]{0:T(128)} %refs_0_.3, s32[8]{0:T(128)} %refs_1_.3, bf16[256,128]{1,0:T(8,128)(2,1)} %refs_2_.2, bf16[256,128]{1,0:T(8,128)(2,1)} %refs_3_.2, f32[160,128]{1,0:T(8,128)} %constant.4.clone.refs_4_, f32[160,128]{1,0:T(8,128)} %constant.5.clone.refs_5_), custom_call_target="tpu_custom_call" | custom-call | tf_op jit(solution)/shard_map/prepare/pallas_call | solution.py:350
  1.8 2.4 %collective-permute-start = (bf16[520,128]{1,0:T(8,128)(2,1)S(1)}, bf16[520,128]{1,0:T(8,128)(2,1)S(1)}, u32[]{:S(2)}, u32[]{:S(2)}) collective-permute-start(bf16[520,128]{1,0:T(8,128)(2,1)S(1)} %prepare.1.refs_6_.rest_0_), channel_id=1, source_target_pairs={{0,4},{1,9},{2,6},{3,11},{4,0},{5,13},{6,2},{7,15},{8,12},{9,1},{1... | collective-permute-start | bytes 399368 | tf_op jit(solution)/shard_map/ppermute | solution.py:364
  4.2 0.3 collective-permute-start.1
  4.4 1.3 %collective-permute-start.2 = (bf16[520,128]{1,0:T(8,128)(2,1)S(1)}, bf16[520,128]{1,0:T(8,128)(2,1)S(1)}, u32[]{:S(2)}, u32[]{:S(2)}) collective-permute-start(bf16[520,128]{1,0:T(8,128)(2,1)S(1)} %prepare.1.refs_6_.rest_0_), channel_id=1, source_target_pairs={{0,2},{1,5},{2,0},{3,7},{4,6},{5,1},{6,4},{7,3},{8,10},{9,13},{10,... | collective-permute-start | bytes 399368 | tf_op jit(solution)/shard_map/ppermute | solution.py:364
  5.7 1.5 %collective-permute-start.3 = (bf16[520,128]{1,0:T(8,128)(2,1)S(1)}, bf16[520,128]{1,0:T(8,128)(2,1)S(1)}, u32[]{:S(2)}, u32[]{:S(2)}) collective-permute-start(bf16[520,128]{1,0:T(8,128)(2,1)S(1)} %prepare.1.refs_6_.rest_0_), channel_id=1, source_target_pairs={{0,1},{1,0},{2,3},{3,2},{4,5},{5,4},{6,7},{7,6},{8,9},{9,8},{10,11... | collective-permute-start | bytes 399368 | tf_op jit(solution)/shard_map/ppermute | solution.py:364
  7.2 1.2 %collective-permute-done.rest_1_ = bf16[520,128]{1,0:T(8,128)(2,1)S(1)} collective-permute-done((bf16[520,128]{1,0:T(8,128)(2,1)S(1)}, bf16[520,128]{1,0:T(8,128)(2,1)S(1)}, u32[]{:S(2)}, u32[]{:S(2)}) %collective-permute-start) | collective-permute-done | bytes 133152 | tf_op jit(solution)/shard_map/ppermute | solution.py:364
  8.5 0.3 collective-permute-start.7
  8.7 0.9 %collective-permute-start.9 = (bf16[520,128]{1,0:T(8,128)(2,1)S(1)}, bf16[520,128]{1,0:T(8,128)(2,1)S(1)}, u32[]{:S(2)}, u32[]{:S(2)}) collective-permute-start(bf16[520,128]{1,0:T(8,128)(2,1)S(1)} %collective-permute-done.rest_1_), channel_id=1, source_target_pairs={{0,8},{1,5},{2,10},{3,7},{4,12},{5,1},{6,14},{7,3},{8,0},{9,13},{1... | collective-permute-start | bytes 399368 | tf_op jit(solution)/shard_map/ppermute | solution.py:364
  9.6 0.0 collective-permute-done.1.rest_2_
  9.6 4.0 %collective-permute-start.4 = (bf16[520,128]{1,0:T(8,128)(2,1)S(1)}, bf16[520,128]{1,0:T(8,128)(2,1)S(1)}, u32[]{:S(2)}, u32[]{:S(2)}) collective-permute-start(bf16[520,128]{1,0:T(8,128)(2,1)S(1)} %collective-permute-done.rest_1_), channel_id=1, source_target_pairs={{0,1},{1,0},{2,3},{3,2},{4,5},{5,4},{6,7},{7,6},{8,9},{9,8},{10,11... | collective-permute-start | bytes 399368 | tf_op jit(solution)/shard_map/ppermute | solution.py:364
  13.6 0.0 collective-permute-done.2.rest_3_
  13.6 0.1 collective-permute-start.5
  13.7 0.0 collective-permute-done.3.rest_4_
  13.7 2.4 %collective-permute-start.10 = (bf16[520,128]{1,0:T(8,128)(2,1)S(1)}, bf16[520,128]{1,0:T(8,128)(2,1)S(1)}, u32[]{:S(2)}, u32[]{:S(2)}) collective-permute-start(bf16[520,128]{1,0:T(8,128)(2,1)S(1)} %collective-permute-done.1.rest_2_), channel_id=1, source_target_pairs={{0,2},{1,5},{2,0},{3,7},{4,6},{5,1},{6,4},{7,3},{8,10},{9,13},{10,... | collective-permute-start | bytes 399368 | tf_op jit(solution)/shard_map/ppermute | solution.py:364
  16.1 0.0 collective-permute-done.7.rest_8_
  16.1 0.1 collective-permute-start.12
  16.2 0.0 collective-permute-done.9.rest_10_
  16.2 1.0 %collective-permute-start.6 = (bf16[520,128]{1,0:T(8,128)(2,1)S(1)}, bf16[520,128]{1,0:T(8,128)(2,1)S(1)}, u32[]{:S(2)}, u32[]{:S(2)}) collective-permute-start(bf16[520,128]{1,0:T(8,128)(2,1)S(1)} %collective-permute-done.2.rest_3_), channel_id=1, source_target_pairs={{0,1},{1,0},{2,3},{3,2},{4,5},{5,4},{6,7},{7,6},{8,9},{9,8},{10,11... | collective-permute-start | bytes 399368 | tf_op jit(solution)/shard_map/ppermute | solution.py:364
  17.2 0.0 collective-permute-done.4.rest_5_
  17.2 0.1 collective-permute-start.8
  17.3 0.0 collective-permute-done.5.rest_6_
  17.3 0.4 %collective-permute-start.11 = (bf16[520,128]{1,0:T(8,128)(2,1)S(1)}, bf16[520,128]{1,0:T(8,128)(2,1)S(1)}, u32[]{:S(2)}, u32[]{:S(2)}) collective-permute-start(bf16[520,128]{1,0:T(8,128)(2,1)S(1)} %collective-permute-done.9.rest_10_), channel_id=1, source_target_pairs={{0,1},{1,0},{2,3},{3,2},{4,5},{5,4},{6,7},{7,6},{8,9},{9,8},{10,11... | collective-permute-start | bytes 399368 | tf_op jit(solution)/shard_map/ppermute | solution.py:364
  17.7 1.0 %collective-permute-done.10.rest_0_ = bf16[520,128]{1,0:T(8,128)(2,1)S(1)} collective-permute-done((bf16[520,128]{1,0:T(8,128)(2,1)S(1)}, bf16[520,128]{1,0:T(8,128)(2,1)S(1)}, u32[]{:S(2)}, u32[]{:S(2)}) %collective-permute-start.10) | collective-permute-done | bytes 133152 | tf_op jit(solution)/shard_map/ppermute | solution.py:364
  18.7 0.4 %collective-permute-start.13 = (bf16[520,128]{1,0:T(8,128)(2,1)S(1)}, bf16[520,128]{1,0:T(8,128)(2,1)S(1)}, u32[]{:S(2)}, u32[]{:S(2)}) collective-permute-start(bf16[520,128]{1,0:T(8,128)(2,1)S(1)} %collective-permute-done.10.rest_0_), channel_id=1, source_target_pairs={{0,1},{1,0},{2,3},{3,2},{4,5},{5,4},{6,7},{7,6},{8,9},{9,8},{10,11... | collective-permute-start | bytes 399368 | tf_op jit(solution)/shard_map/ppermute | solution.py:364
  19.1 2.1 %collective-permute-done.12.rest_2_ = bf16[520,128]{1,0:T(8,128)(2,1)S(1)} collective-permute-done((bf16[520,128]{1,0:T(8,128)(2,1)S(1)}, bf16[520,128]{1,0:T(8,128)(2,1)S(1)}, u32[]{:S(2)}, u32[]{:S(2)}) %collective-permute-start.12) | collective-permute-done | bytes 133152 | tf_op jit(solution)/shard_map/ppermute | solution.py:364
  21.2 2.1 %collective-permute-start.14 = (bf16[520,128]{1,0:T(8,128)(2,1)S(1)}, bf16[520,128]{1,0:T(8,128)(2,1)S(1)}, u32[]{:S(2)}, u32[]{:S(2)}) collective-permute-start(bf16[520,128]{1,0:T(8,128)(2,1)S(1)} %collective-permute-done.12.rest_2_), channel_id=1, source_target_pairs={{0,1},{1,0},{2,3},{3,2},{4,5},{5,4},{6,7},{7,6},{8,9},{9,8},{10,11... | collective-permute-start | bytes 399368 | tf_op jit(solution)/shard_map/ppermute | solution.py:364
  23.3 1.9 %early.1 = (s32[8,128]{1,0:T(8,128)S(1)}, bf16[1536,128]{1,0:T(8,128)(2,1)S(1)}, f32[1536,128]{1,0:T(8,128)S(1)}, f32[1536,128]{1,0:T(8,128)S(1)}, f32[1536,128]{1,0:T(8,128)S(1)}) custom-call(s32[2]{0:T(128)} %refs_0_.3, s32[8]{0:T(128)} %refs_1_.3, s32[32]{0:T(128)} %refs_2_.3, bf16[256,768]{1,0:T(8,128)(2,1)} %refs_3_.3, ...), custom_call_target="tpu_custom_call" | custom-call | tf_op jit(solution)/shard_map/early/pallas_call | solution.py:376
  25.3 0.0 collective-permute-done.6.rest_7_
  25.3 3.5 %shard_map.95 = (f32[1536,128]{1,0:T(8,128)S(1)}, f32[1536,128]{1,0:T(8,128)S(1)}, f32[1536,128]{1,0:T(8,128)S(1)}, bf16[2,128,256]{2,1,0:T(8,128)(2,1)}) custom-call(s32[8,128]{1,0:T(8,128)S(1)} %get-tuple-element.17.info, bf16[1536,128]{1,0:T(8,128)(2,1)S(1)} %get-tuple-element.18.q_rot, ...), custom_call_target="tpu_custom_call", output_to_operand_aliasing={{0}: (2, {}), {1}: (3, {}), {2}: (4, {})} | custom-call | tf_op jit(solution)/shard_map/pallas_call | solution.py:421
  28.8 1.6 %shard_map.96 = (f32[1536,128]{1,0:T(8,128)S(1)}, f32[1536,128]{1,0:T(8,128)S(1)}, f32[1536,128]{1,0:T(8,128)S(1)}, bf16[2,128,256]{2,1,0:T(8,128)(2,1)}) custom-call(s32[8,128]{1,0:T(8,128)S(1)} %get-tuple-element.17.info, bf16[1536,128]{1,0:T(8,128)(2,1)S(1)} %get-tuple-element.18.q_rot, ...), custom_call_target="tpu_custom_call", output_to_operand_aliasing={{0}: (2, {}), {1}: (3, {}), {2}: (4, {}), {3}: (8, {})} | custom-call | tf_op jit(solution)/shard_map/pallas_call | solution.py:421
  30.4 0.0 collective-permute-done.13.rest_0_
  30.5 1.9 %shard_map.97 = (f32[1536,128]{1,0:T(8,128)S(1)}, f32[1536,128]{1,0:T(8,128)S(1)}, f32[1536,128]{1,0:T(8,128)S(1)}, bf16[256,768]{1,0:T(8,128)(2,1)}, bf16[2,128,256]{2,1,0:T(8,128)(2,1)}) custom-call(s32[8,128]{1,0:T(8,128)S(1)} %get-tuple-element.17.info, ...), custom_call_target="tpu_custom_call", output_to_operand_aliasing={{0}: (2, {}), {1}: (3, {}), {2}: (4, {}), {4}: (7, {})} | custom-call | tf_op jit(solution)/shard_map/pallas_call | solution.py:421
  (3 shorter events, 0.0 us)
Async XLA Ops:
  1.8 6.7 %collective-permute-start = (bf16[520,128]{1,0:T(8,128)(2,1)S(1)}, bf16[520,128]{1,0:T(8,128)(2,1)S(1)}, u32[]{:S(2)}, u32[]{:S(2)}) collective-permute-start(bf16[520,128]{1,0:T(8,128)(2,1)S(1)} %prepare.1.refs_6_.rest_0_), channel_id=1, source_target_pairs={{0,4},{1,9},{2,6},{3,11},{4,0},{5,13},{6,2},{7,15},{8,12},{9,1},{1... | collective-permute-start | bytes 399368 | tf_op jit(solution)/shard_map/ppermute | solution.py:364
  4.2 5.5 %collective-permute-start.1 = (bf16[520,128]{1,0:T(8,128)(2,1)S(1)}, bf16[520,128]{1,0:T(8,128)(2,1)S(1)}, u32[]{:S(2)}, u32[]{:S(2)}) collective-permute-start(bf16[520,128]{1,0:T(8,128)(2,1)S(1)} %prepare.1.refs_6_.rest_0_), channel_id=1, source_target_pairs={{0,8},{1,3},{2,10},{3,1},{4,12},{5,7},{6,14},{7,5},{8,0},{9,11},{1... | collective-permute-start | bytes 399368 | tf_op jit(solution)/shard_map/ppermute | solution.py:364
  4.4 9.2 %collective-permute-start.2 = (bf16[520,128]{1,0:T(8,128)(2,1)S(1)}, bf16[520,128]{1,0:T(8,128)(2,1)S(1)}, u32[]{:S(2)}, u32[]{:S(2)}) collective-permute-start(bf16[520,128]{1,0:T(8,128)(2,1)S(1)} %prepare.1.refs_6_.rest_0_), channel_id=1, source_target_pairs={{0,2},{1,5},{2,0},{3,7},{4,6},{5,1},{6,4},{7,3},{8,10},{9,13},{10,... | collective-permute-start | bytes 399368 | tf_op jit(solution)/shard_map/ppermute | solution.py:364
  5.7 8.0 %collective-permute-start.3 = (bf16[520,128]{1,0:T(8,128)(2,1)S(1)}, bf16[520,128]{1,0:T(8,128)(2,1)S(1)}, u32[]{:S(2)}, u32[]{:S(2)}) collective-permute-start(bf16[520,128]{1,0:T(8,128)(2,1)S(1)} %prepare.1.refs_6_.rest_0_), channel_id=1, source_target_pairs={{0,1},{1,0},{2,3},{3,2},{4,5},{5,4},{6,7},{7,6},{8,9},{9,8},{10,11... | collective-permute-start | bytes 399368 | tf_op jit(solution)/shard_map/ppermute | solution.py:364
  8.5 7.7 %collective-permute-start.7 = (bf16[520,128]{1,0:T(8,128)(2,1)S(1)}, bf16[520,128]{1,0:T(8,128)(2,1)S(1)}, u32[]{:S(2)}, u32[]{:S(2)}) collective-permute-start(bf16[520,128]{1,0:T(8,128)(2,1)S(1)} %collective-permute-done.rest_1_), channel_id=1, source_target_pairs={{0,2},{1,3},{2,0},{3,1},{4,6},{5,7},{6,4},{7,5},{8,10},{9,11},{10,... | collective-permute-start | bytes 399368 | tf_op jit(solution)/shard_map/ppermute | solution.py:364
  8.7 7.5 %collective-permute-start.9 = (bf16[520,128]{1,0:T(8,128)(2,1)S(1)}, bf16[520,128]{1,0:T(8,128)(2,1)S(1)}, u32[]{:S(2)}, u32[]{:S(2)}) collective-permute-start(bf16[520,128]{1,0:T(8,128)(2,1)S(1)} %collective-permute-done.rest_1_), channel_id=1, source_target_pairs={{0,8},{1,5},{2,10},{3,7},{4,12},{5,1},{6,14},{7,3},{8,0},{9,13},{1... | collective-permute-start | bytes 399368 | tf_op jit(solution)/shard_map/ppermute | solution.py:364
  9.6 7.6 %collective-permute-start.4 = (bf16[520,128]{1,0:T(8,128)(2,1)S(1)}, bf16[520,128]{1,0:T(8,128)(2,1)S(1)}, u32[]{:S(2)}, u32[]{:S(2)}) collective-permute-start(bf16[520,128]{1,0:T(8,128)(2,1)S(1)} %collective-permute-done.rest_1_), channel_id=1, source_target_pairs={{0,1},{1,0},{2,3},{3,2},{4,5},{5,4},{6,7},{7,6},{8,9},{9,8},{10,11... | collective-permute-start | bytes 399368 | tf_op jit(solution)/shard_map/ppermute | solution.py:364
  13.6 3.7 %collective-permute-start.5 = (bf16[520,128]{1,0:T(8,128)(2,1)S(1)}, bf16[520,128]{1,0:T(8,128)(2,1)S(1)}, u32[]{:S(2)}, u32[]{:S(2)}) collective-permute-start(bf16[520,128]{1,0:T(8,128)(2,1)S(1)} %collective-permute-done.1.rest_2_), channel_id=1, source_target_pairs={{0,1},{1,0},{2,3},{3,2},{4,5},{5,4},{6,7},{7,6},{8,9},{9,8},{10,11... | collective-permute-start | bytes 399368 | tf_op jit(solution)/shard_map/ppermute | solution.py:364
  13.7 5.0 %collective-permute-start.10 = (bf16[520,128]{1,0:T(8,128)(2,1)S(1)}, bf16[520,128]{1,0:T(8,128)(2,1)S(1)}, u32[]{:S(2)}, u32[]{:S(2)}) collective-permute-start(bf16[520,128]{1,0:T(8,128)(2,1)S(1)} %collective-permute-done.1.rest_2_), channel_id=1, source_target_pairs={{0,2},{1,5},{2,0},{3,7},{4,6},{5,1},{6,4},{7,3},{8,10},{9,13},{10,... | collective-permute-start | bytes 399368 | tf_op jit(solution)/shard_map/ppermute | solution.py:364
  16.1 5.1 %collective-permute-start.12 = (bf16[520,128]{1,0:T(8,128)(2,1)S(1)}, bf16[520,128]{1,0:T(8,128)(2,1)S(1)}, u32[]{:S(2)}, u32[]{:S(2)}) collective-permute-start(bf16[520,128]{1,0:T(8,128)(2,1)S(1)} %collective-permute-done.7.rest_8_), channel_id=1, source_target_pairs={{0,8},{1,5},{2,10},{3,7},{4,12},{5,1},{6,14},{7,3},{8,0},{9,13},{1... | collective-permute-start | bytes 399368 | tf_op jit(solution)/shard_map/ppermute | solution.py:364
  16.2 9.1 %collective-permute-start.6 = (bf16[520,128]{1,0:T(8,128)(2,1)S(1)}, bf16[520,128]{1,0:T(8,128)(2,1)S(1)}, u32[]{:S(2)}, u32[]{:S(2)}) collective-permute-start(bf16[520,128]{1,0:T(8,128)(2,1)S(1)} %collective-permute-done.2.rest_3_), channel_id=1, source_target_pairs={{0,1},{1,0},{2,3},{3,2},{4,5},{5,4},{6,7},{7,6},{8,9},{9,8},{10,11... | collective-permute-start | bytes 399368 | tf_op jit(solution)/shard_map/ppermute | solution.py:364
  17.2 8.1 %collective-permute-start.8 = (bf16[520,128]{1,0:T(8,128)(2,1)S(1)}, bf16[520,128]{1,0:T(8,128)(2,1)S(1)}, u32[]{:S(2)}, u32[]{:S(2)}) collective-permute-start(bf16[520,128]{1,0:T(8,128)(2,1)S(1)} %collective-permute-done.7.rest_8_), channel_id=1, source_target_pairs={{0,1},{1,0},{2,3},{3,2},{4,5},{5,4},{6,7},{7,6},{8,9},{9,8},{10,11... | collective-permute-start | bytes 399368 | tf_op jit(solution)/shard_map/ppermute | solution.py:364
  17.3 11.5 %collective-permute-start.11 = (bf16[520,128]{1,0:T(8,128)(2,1)S(1)}, bf16[520,128]{1,0:T(8,128)(2,1)S(1)}, u32[]{:S(2)}, u32[]{:S(2)}) collective-permute-start(bf16[520,128]{1,0:T(8,128)(2,1)S(1)} %collective-permute-done.9.rest_10_), channel_id=1, source_target_pairs={{0,1},{1,0},{2,3},{3,2},{4,5},{5,4},{6,7},{7,6},{8,9},{9,8},{10,11... | collective-permute-start | bytes 399368 | tf_op jit(solution)/shard_map/ppermute | solution.py:364
  18.7 11.7 %collective-permute-start.13 = (bf16[520,128]{1,0:T(8,128)(2,1)S(1)}, bf16[520,128]{1,0:T(8,128)(2,1)S(1)}, u32[]{:S(2)}, u32[]{:S(2)}) collective-permute-start(bf16[520,128]{1,0:T(8,128)(2,1)S(1)} %collective-permute-done.10.rest_0_), channel_id=1, source_target_pairs={{0,1},{1,0},{2,3},{3,2},{4,5},{5,4},{6,7},{7,6},{8,9},{9,8},{10,11... | collective-permute-start | bytes 399368 | tf_op jit(solution)/shard_map/ppermute | solution.py:364
  21.2 9.2 %collective-permute-start.14 = (bf16[520,128]{1,0:T(8,128)(2,1)S(1)}, bf16[520,128]{1,0:T(8,128)(2,1)S(1)}, u32[]{:S(2)}, u32[]{:S(2)}) collective-permute-start(bf16[520,128]{1,0:T(8,128)(2,1)S(1)} %collective-permute-done.12.rest_2_), channel_id=1, source_target_pairs={{0,1},{1,0},{2,3},{3,2},{4,5},{5,4},{6,7},{7,6},{8,9},{9,8},{10,11... | collective-permute-start | bytes 399368 | tf_op jit(solution)/shard_map/ppermute | solution.py:364

commit v4 on v3

--- a/solution.py
+++ b/solution.py
@@ -313,17 +313,17 @@
 
 
 ROUTE = (
-    ("v1", "o", 4, 8),
-    ("v2", "o", 8, 2),
-    ("v3", "o", 2, 4),
+    ("v1", "o", 8, 8),
+    ("v2", "o", 2, 4),
+    ("v3", "o", 4, 2),
     ("co", "o", 1, 1),
-    ("v4", "v1", 2, 2),
-    ("v5", "v1", 8, 4),
-    ("v6", "v2", 2, 4),
+    ("v4", "v1", 2, 4),
+    ("v5", "v1", 4, 2),
+    ("v6", "v3", 2, 4),
     ("cv3", "v3", 1, 1),
     ("cv1", "v1", 1, 1),
     ("cv2", "v2", 1, 1),
-    ("v7", "v4", 8, 4),
+    ("v7", "v4", 4, 2),
     ("cv4", "v4", 1, 1),
     ("cv5", "v5", 1, 1),
     ("cv6", "v6", 1, 1),

time: 32.7 us -> 32.3 us (0.988)
  waiting for transfers between devices: 4.38 us -> 3.56 us
    ppermute x15, waiting for transfers between devices: 4.38 us -> 3.56 us  [swap(): lax.ppermute(x, 'seq', [(i, i ^ (odd if i % 2 else even)) for i in range(...]
  transfers between devices with their start and end apart: 15 -> 15, of which waited for: 3 -> 2; matrix products, arithmetic and copies ran while one was open for 0% -> 0% of each run, Pallas kernels for 22% -> 22%
where the time goes in v4:
time: 32.3 us; the launch traced here: 32.2 us
  starting transfers between devices  17.3 us (54%)
  Pallas kernels  10.4 us (32%)
  waiting for transfers between devices  3.56 us (11%)
  between operations  0.88 us (3%)
    ppermute x15, starting transfers between devices, swap(): lax.ppermute(x, 'seq', [(i, i ^ (odd if i % 2 else even)) for i in range(...  17.3 us
    pallas_call x3, Pallas kernels, take(): pl.pallas_call(functools.partial(absorb, per_rank, len(pieces), pages is...  7.29 us
    ppermute x15, waiting for transfers between devices, swap(): lax.ppermute(x, 'seq', [(i, i ^ (odd if i % 2 else even)) for i in range(...  3.56 us
    pallas_call x1, Pallas kernels, plan(): pl.pallas_call(functools.partial(early, spans), out_shape=(pltpu.VMEM((-(...  1.94 us
    pallas_call x1, Pallas kernels, plan(): pl.pallas_call(functools.partial(prepare, spans), out_shape=pltpu.VMEM((b...  1.16 us
  transfers between devices with their start and end apart: 15, of which 2 were waited for; matrix products, arithmetic and copies ran while one was open for 0% of the time, Pallas kernels for 22%

profile of v4, /device:TPU:7, one launch (start us, length us, event | category | flops | bytes accessed | tf_op | source)
XLA Modules:
  0.0 32.2 jit_solution(17571960071362779357)
XLA Ops:
  0.6 1.2 %prepare.1.refs_6_.rest_0_ = bf16[520,128]{1,0:T(8,128)(2,1)S(1)} custom-call(s32[2]{0:T(128)} %refs_0_.3, s32[8]{0:T(128)} %refs_1_.3, bf16[256,128]{1,0:T(8,128)(2,1)} %refs_2_.2, bf16[256,128]{1,0:T(8,128)(2,1)} %refs_3_.2, f32[160,128]{1,0:T(8,128)} %constant.4.clone.refs_4_, f32[160,128]{1,0:T(8,128)} %constant.5.clone.refs_5_), custom_call_target="tpu_custom_call" | custom-call | tf_op jit(solution)/shard_map/prepare/pallas_call | solution.py:350
  1.8 2.4 %collective-permute-start = (bf16[520,128]{1,0:T(8,128)(2,1)S(1)}, bf16[520,128]{1,0:T(8,128)(2,1)S(1)}, u32[]{:S(2)}, u32[]{:S(2)}) collective-permute-start(bf16[520,128]{1,0:T(8,128)(2,1)S(1)} %prepare.1.refs_6_.rest_0_), channel_id=1, source_target_pairs={{0,8},{1,9},{2,10},{3,11},{4,12},{5,13},{6,14},{7,15},{8,0},{9,1},... | collective-permute-start | bytes 399368 | tf_op jit(solution)/shard_map/ppermute | solution.py:364
  4.2 0.3 collective-permute-start.2
  4.4 1.3 %collective-permute-start.1 = (bf16[520,128]{1,0:T(8,128)(2,1)S(1)}, bf16[520,128]{1,0:T(8,128)(2,1)S(1)}, u32[]{:S(2)}, u32[]{:S(2)}) collective-permute-start(bf16[520,128]{1,0:T(8,128)(2,1)S(1)} %prepare.1.refs_6_.rest_0_), channel_id=1, source_target_pairs={{0,2},{1,5},{2,0},{3,7},{4,6},{5,1},{6,4},{7,3},{8,10},{9,13},{10,... | collective-permute-start | bytes 399368 | tf_op jit(solution)/shard_map/ppermute | solution.py:364
  5.7 1.5 %collective-permute-start.3 = (bf16[520,128]{1,0:T(8,128)(2,1)S(1)}, bf16[520,128]{1,0:T(8,128)(2,1)S(1)}, u32[]{:S(2)}, u32[]{:S(2)}) collective-permute-start(bf16[520,128]{1,0:T(8,128)(2,1)S(1)} %prepare.1.refs_6_.rest_0_), channel_id=1, source_target_pairs={{0,1},{1,0},{2,3},{3,2},{4,5},{5,4},{6,7},{7,6},{8,9},{9,8},{10,11... | collective-permute-start | bytes 399368 | tf_op jit(solution)/shard_map/ppermute | solution.py:364
  7.2 2.4 %collective-permute-done.rest_1_ = bf16[520,128]{1,0:T(8,128)(2,1)S(1)} collective-permute-done((bf16[520,128]{1,0:T(8,128)(2,1)S(1)}, bf16[520,128]{1,0:T(8,128)(2,1)S(1)}, u32[]{:S(2)}, u32[]{:S(2)}) %collective-permute-start) | collective-permute-done | bytes 133152 | tf_op jit(solution)/shard_map/ppermute | solution.py:364
  9.6 1.8 %collective-permute-start.7 = (bf16[520,128]{1,0:T(8,128)(2,1)S(1)}, bf16[520,128]{1,0:T(8,128)(2,1)S(1)}, u32[]{:S(2)}, u32[]{:S(2)}) collective-permute-start(bf16[520,128]{1,0:T(8,128)(2,1)S(1)} %collective-permute-done.rest_1_), channel_id=1, source_target_pairs={{0,2},{1,5},{2,0},{3,7},{4,6},{5,1},{6,4},{7,3},{8,10},{9,13},{10,... | collective-permute-start | bytes 399368 | tf_op jit(solution)/shard_map/ppermute | solution.py:364
  11.5 0.3 collective-permute-start.9
  11.8 0.0 collective-permute-done.2.rest_3_
  11.8 1.1 %collective-permute-start.4 = (bf16[520,128]{1,0:T(8,128)(2,1)S(1)}, bf16[520,128]{1,0:T(8,128)(2,1)S(1)}, u32[]{:S(2)}, u32[]{:S(2)}) collective-permute-start(bf16[520,128]{1,0:T(8,128)(2,1)S(1)} %collective-permute-done.rest_1_), channel_id=1, source_target_pairs={{0,1},{1,0},{2,3},{3,2},{4,5},{5,4},{6,7},{7,6},{8,9},{9,8},{10,11... | collective-permute-start | bytes 399368 | tf_op jit(solution)/shard_map/ppermute | solution.py:364
  12.8 0.0 collective-permute-done.1.rest_2_
  12.8 0.1 collective-permute-start.6
  12.9 0.0 collective-permute-done.3.rest_4_
  12.9 1.1 %collective-permute-start.10 = (bf16[520,128]{1,0:T(8,128)(2,1)S(1)}, bf16[520,128]{1,0:T(8,128)(2,1)S(1)}, u32[]{:S(2)}, u32[]{:S(2)}) collective-permute-start(bf16[520,128]{1,0:T(8,128)(2,1)S(1)} %collective-permute-done.2.rest_3_), channel_id=1, source_target_pairs={{0,2},{1,5},{2,0},{3,7},{4,6},{5,1},{6,4},{7,3},{8,10},{9,13},{10,... | collective-permute-start | bytes 399368 | tf_op jit(solution)/shard_map/ppermute | solution.py:364
  14.0 0.0 collective-permute-done.7.rest_8_
  14.0 1.2 %collective-permute-start.12 = (bf16[520,128]{1,0:T(8,128)(2,1)S(1)}, bf16[520,128]{1,0:T(8,128)(2,1)S(1)}, u32[]{:S(2)}, u32[]{:S(2)}) collective-permute-start(bf16[520,128]{1,0:T(8,128)(2,1)S(1)} %collective-permute-done.7.rest_8_), channel_id=1, source_target_pairs={{0,4},{1,3},{2,6},{3,1},{4,0},{5,7},{6,2},{7,5},{8,12},{9,11},{10,... | collective-permute-start | bytes 399368 | tf_op jit(solution)/shard_map/ppermute | solution.py:364
  15.2 1.1 %collective-permute-done.9.rest_10_ = bf16[520,128]{1,0:T(8,128)(2,1)S(1)} collective-permute-done((bf16[520,128]{1,0:T(8,128)(2,1)S(1)}, bf16[520,128]{1,0:T(8,128)(2,1)S(1)}, u32[]{:S(2)}, u32[]{:S(2)}) %collective-permute-start.9) | collective-permute-done | bytes 133152 | tf_op jit(solution)/shard_map/ppermute | solution.py:364
  16.4 2.0 %collective-permute-start.5 = (bf16[520,128]{1,0:T(8,128)(2,1)S(1)}, bf16[520,128]{1,0:T(8,128)(2,1)S(1)}, u32[]{:S(2)}, u32[]{:S(2)}) collective-permute-start(bf16[520,128]{1,0:T(8,128)(2,1)S(1)} %collective-permute-done.1.rest_2_), channel_id=1, source_target_pairs={{0,1},{1,0},{2,3},{3,2},{4,5},{5,4},{6,7},{7,6},{8,9},{9,8},{10,11... | collective-permute-start | bytes 399368 | tf_op jit(solution)/shard_map/ppermute | solution.py:364
  18.4 0.0 collective-permute-done.4.rest_5_
  18.4 0.0 collective-permute-start.8
  18.4 0.0 collective-permute-done.6.rest_7_
  18.4 0.5 %collective-permute-start.11 = (bf16[520,128]{1,0:T(8,128)(2,1)S(1)}, bf16[520,128]{1,0:T(8,128)(2,1)S(1)}, u32[]{:S(2)}, u32[]{:S(2)}) collective-permute-start(bf16[520,128]{1,0:T(8,128)(2,1)S(1)} %collective-permute-done.9.rest_10_), channel_id=1, source_target_pairs={{0,1},{1,0},{2,3},{3,2},{4,5},{5,4},{6,7},{7,6},{8,9},{9,8},{10,11... | collective-permute-start | bytes 399368 | tf_op jit(solution)/shard_map/ppermute | solution.py:364
  18.9 1.4 %collective-permute-start.13 = (bf16[520,128]{1,0:T(8,128)(2,1)S(1)}, bf16[520,128]{1,0:T(8,128)(2,1)S(1)}, u32[]{:S(2)}, u32[]{:S(2)}) collective-permute-start(bf16[520,128]{1,0:T(8,128)(2,1)S(1)} %collective-permute-done.10.rest_0_), channel_id=1, source_target_pairs={{0,1},{1,0},{2,3},{3,2},{4,5},{5,4},{6,7},{7,6},{8,9},{9,8},{10,11... | collective-permute-start | bytes 399368 | tf_op jit(solution)/shard_map/ppermute | solution.py:364
  20.3 0.0 collective-permute-done.12.rest_2_
  20.3 2.4 %collective-permute-start.14 = (bf16[520,128]{1,0:T(8,128)(2,1)S(1)}, bf16[520,128]{1,0:T(8,128)(2,1)S(1)}, u32[]{:S(2)}, u32[]{:S(2)}) collective-permute-start(bf16[520,128]{1,0:T(8,128)(2,1)S(1)} %collective-permute-done.12.rest_2_), channel_id=1, source_target_pairs={{0,1},{1,0},{2,3},{3,2},{4,5},{5,4},{6,7},{7,6},{8,9},{9,8},{10,11... | collective-permute-start | bytes 399368 | tf_op jit(solution)/shard_map/ppermute | solution.py:364
  22.7 1.9 %early.1 = (s32[8,128]{1,0:T(8,128)S(1)}, bf16[1536,128]{1,0:T(8,128)(2,1)S(1)}, f32[1536,128]{1,0:T(8,128)S(1)}, f32[1536,128]{1,0:T(8,128)S(1)}, f32[1536,128]{1,0:T(8,128)S(1)}) custom-call(s32[2]{0:T(128)} %refs_0_.3, s32[8]{0:T(128)} %refs_1_.3, s32[32]{0:T(128)} %refs_2_.3, bf16[256,768]{1,0:T(8,128)(2,1)} %refs_3_.3, ...), custom_call_target="tpu_custom_call" | custom-call | tf_op jit(solution)/shard_map/early/pallas_call | solution.py:376
  24.7 0.0 collective-permute-done.8.rest_9_
  24.7 3.4 %shard_map.95 = (f32[1536,128]{1,0:T(8,128)S(1)}, f32[1536,128]{1,0:T(8,128)S(1)}, f32[1536,128]{1,0:T(8,128)S(1)}, bf16[2,128,256]{2,1,0:T(8,128)(2,1)}) custom-call(s32[8,128]{1,0:T(8,128)S(1)} %get-tuple-element.17.info, bf16[1536,128]{1,0:T(8,128)(2,1)S(1)} %get-tuple-element.18.q_rot, ...), custom_call_target="tpu_custom_call", output_to_operand_aliasing={{0}: (2, {}), {1}: (3, {}), {2}: (4, {})} | custom-call | tf_op jit(solution)/shard_map/pallas_call | solution.py:421
  28.1 0.0 collective-permute-done.11.rest_1_
  28.1 1.6 %shard_map.96 = (f32[1536,128]{1,0:T(8,128)S(1)}, f32[1536,128]{1,0:T(8,128)S(1)}, f32[1536,128]{1,0:T(8,128)S(1)}, bf16[2,128,256]{2,1,0:T(8,128)(2,1)}) custom-call(s32[8,128]{1,0:T(8,128)S(1)} %get-tuple-element.17.info, bf16[1536,128]{1,0:T(8,128)(2,1)S(1)} %get-tuple-element.18.q_rot, ...), custom_call_target="tpu_custom_call", output_to_operand_aliasing={{0}: (2, {}), {1}: (3, {}), {2}: (4, {}), {3}: (8, {})} | custom-call | tf_op jit(solution)/shard_map/pallas_call | solution.py:421
  29.7 0.0 collective-permute-done.13.rest_0_
  29.7 2.3 %shard_map.97 = (f32[1536,128]{1,0:T(8,128)S(1)}, f32[1536,128]{1,0:T(8,128)S(1)}, f32[1536,128]{1,0:T(8,128)S(1)}, bf16[256,768]{1,0:T(8,128)(2,1)}, bf16[2,128,256]{2,1,0:T(8,128)(2,1)}) custom-call(s32[8,128]{1,0:T(8,128)S(1)} %get-tuple-element.17.info, ...), custom_call_target="tpu_custom_call", output_to_operand_aliasing={{0}: (2, {}), {1}: (3, {}), {2}: (4, {}), {4}: (7, {})} | custom-call | tf_op jit(solution)/shard_map/pallas_call | solution.py:421
  (3 shorter events, 0.0 us)
Async XLA Ops:
  1.8 7.9 %collective-permute-start = (bf16[520,128]{1,0:T(8,128)(2,1)S(1)}, bf16[520,128]{1,0:T(8,128)(2,1)S(1)}, u32[]{:S(2)}, u32[]{:S(2)}) collective-permute-start(bf16[520,128]{1,0:T(8,128)(2,1)S(1)} %prepare.1.refs_6_.rest_0_), channel_id=1, source_target_pairs={{0,8},{1,9},{2,10},{3,11},{4,12},{5,13},{6,14},{7,15},{8,0},{9,1},... | collective-permute-start | bytes 399368 | tf_op jit(solution)/shard_map/ppermute | solution.py:364
  4.2 7.6 %collective-permute-start.2 = (bf16[520,128]{1,0:T(8,128)(2,1)S(1)}, bf16[520,128]{1,0:T(8,128)(2,1)S(1)}, u32[]{:S(2)}, u32[]{:S(2)}) collective-permute-start(bf16[520,128]{1,0:T(8,128)(2,1)S(1)} %prepare.1.refs_6_.rest_0_), channel_id=1, source_target_pairs={{0,4},{1,3},{2,6},{3,1},{4,0},{5,7},{6,2},{7,5},{8,12},{9,11},{10,... | collective-permute-start | bytes 399368 | tf_op jit(solution)/shard_map/ppermute | solution.py:364
  4.4 8.4 %collective-permute-start.1 = (bf16[520,128]{1,0:T(8,128)(2,1)S(1)}, bf16[520,128]{1,0:T(8,128)(2,1)S(1)}, u32[]{:S(2)}, u32[]{:S(2)}) collective-permute-start(bf16[520,128]{1,0:T(8,128)(2,1)S(1)} %prepare.1.refs_6_.rest_0_), channel_id=1, source_target_pairs={{0,2},{1,5},{2,0},{3,7},{4,6},{5,1},{6,4},{7,3},{8,10},{9,13},{10,... | collective-permute-start | bytes 399368 | tf_op jit(solution)/shard_map/ppermute | solution.py:364
  5.7 7.2 %collective-permute-start.3 = (bf16[520,128]{1,0:T(8,128)(2,1)S(1)}, bf16[520,128]{1,0:T(8,128)(2,1)S(1)}, u32[]{:S(2)}, u32[]{:S(2)}) collective-permute-start(bf16[520,128]{1,0:T(8,128)(2,1)S(1)} %prepare.1.refs_6_.rest_0_), channel_id=1, source_target_pairs={{0,1},{1,0},{2,3},{3,2},{4,5},{5,4},{6,7},{7,6},{8,9},{9,8},{10,11... | collective-permute-start | bytes 399368 | tf_op jit(solution)/shard_map/ppermute | solution.py:364
  9.6 4.4 %collective-permute-start.7 = (bf16[520,128]{1,0:T(8,128)(2,1)S(1)}, bf16[520,128]{1,0:T(8,128)(2,1)S(1)}, u32[]{:S(2)}, u32[]{:S(2)}) collective-permute-start(bf16[520,128]{1,0:T(8,128)(2,1)S(1)} %collective-permute-done.rest_1_), channel_id=1, source_target_pairs={{0,2},{1,5},{2,0},{3,7},{4,6},{5,1},{6,4},{7,3},{8,10},{9,13},{10,... | collective-permute-start | bytes 399368 | tf_op jit(solution)/shard_map/ppermute | solution.py:364
  11.5 4.9 %collective-permute-start.9 = (bf16[520,128]{1,0:T(8,128)(2,1)S(1)}, bf16[520,128]{1,0:T(8,128)(2,1)S(1)}, u32[]{:S(2)}, u32[]{:S(2)}) collective-permute-start(bf16[520,128]{1,0:T(8,128)(2,1)S(1)} %collective-permute-done.rest_1_), channel_id=1, source_target_pairs={{0,4},{1,3},{2,6},{3,1},{4,0},{5,7},{6,2},{7,5},{8,12},{9,11},{10,... | collective-permute-start | bytes 399368 | tf_op jit(solution)/shard_map/ppermute | solution.py:364
  11.8 6.6 %collective-permute-start.4 = (bf16[520,128]{1,0:T(8,128)(2,1)S(1)}, bf16[520,128]{1,0:T(8,128)(2,1)S(1)}, u32[]{:S(2)}, u32[]{:S(2)}) collective-permute-start(bf16[520,128]{1,0:T(8,128)(2,1)S(1)} %collective-permute-done.rest_1_), channel_id=1, source_target_pairs={{0,1},{1,0},{2,3},{3,2},{4,5},{5,4},{6,7},{7,6},{8,9},{9,8},{10,11... | collective-permute-start | bytes 399368 | tf_op jit(solution)/shard_map/ppermute | solution.py:364
  12.8 5.6 %collective-permute-start.6 = (bf16[520,128]{1,0:T(8,128)(2,1)S(1)}, bf16[520,128]{1,0:T(8,128)(2,1)S(1)}, u32[]{:S(2)}, u32[]{:S(2)}) collective-permute-start(bf16[520,128]{1,0:T(8,128)(2,1)S(1)} %collective-permute-done.2.rest_3_), channel_id=1, source_target_pairs={{0,1},{1,0},{2,3},{3,2},{4,5},{5,4},{6,7},{7,6},{8,9},{9,8},{10,11... | collective-permute-start | bytes 399368 | tf_op jit(solution)/shard_map/ppermute | solution.py:364
  12.9 6.0 %collective-permute-start.10 = (bf16[520,128]{1,0:T(8,128)(2,1)S(1)}, bf16[520,128]{1,0:T(8,128)(2,1)S(1)}, u32[]{:S(2)}, u32[]{:S(2)}) collective-permute-start(bf16[520,128]{1,0:T(8,128)(2,1)S(1)} %collective-permute-done.2.rest_3_), channel_id=1, source_target_pairs={{0,2},{1,5},{2,0},{3,7},{4,6},{5,1},{6,4},{7,3},{8,10},{9,13},{10,... | collective-permute-start | bytes 399368 | tf_op jit(solution)/shard_map/ppermute | solution.py:364
  14.0 6.2 %collective-permute-start.12 = (bf16[520,128]{1,0:T(8,128)(2,1)S(1)}, bf16[520,128]{1,0:T(8,128)(2,1)S(1)}, u32[]{:S(2)}, u32[]{:S(2)}) collective-permute-start(bf16[520,128]{1,0:T(8,128)(2,1)S(1)} %collective-permute-done.7.rest_8_), channel_id=1, source_target_pairs={{0,4},{1,3},{2,6},{3,1},{4,0},{5,7},{6,2},{7,5},{8,12},{9,11},{10,... | collective-permute-start | bytes 399368 | tf_op jit(solution)/shard_map/ppermute | solution.py:364
  16.4 8.3 %collective-permute-start.5 = (bf16[520,128]{1,0:T(8,128)(2,1)S(1)}, bf16[520,128]{1,0:T(8,128)(2,1)S(1)}, u32[]{:S(2)}, u32[]{:S(2)}) collective-permute-start(bf16[520,128]{1,0:T(8,128)(2,1)S(1)} %collective-permute-done.1.rest_2_), channel_id=1, source_target_pairs={{0,1},{1,0},{2,3},{3,2},{4,5},{5,4},{6,7},{7,6},{8,9},{9,8},{10,11... | collective-permute-start | bytes 399368 | tf_op jit(solution)/shard_map/ppermute | solution.py:364
  18.4 6.3 %collective-permute-start.8 = (bf16[520,128]{1,0:T(8,128)(2,1)S(1)}, bf16[520,128]{1,0:T(8,128)(2,1)S(1)}, u32[]{:S(2)}, u32[]{:S(2)}) collective-permute-start(bf16[520,128]{1,0:T(8,128)(2,1)S(1)} %collective-permute-done.7.rest_8_), channel_id=1, source_target_pairs={{0,1},{1,0},{2,3},{3,2},{4,5},{5,4},{6,7},{7,6},{8,9},{9,8},{10,11... | collective-permute-start | bytes 399368 | tf_op jit(solution)/shard_map/ppermute | solution.py:364
  18.4 9.7 %collective-permute-start.11 = (bf16[520,128]{1,0:T(8,128)(2,1)S(1)}, bf16[520,128]{1,0:T(8,128)(2,1)S(1)}, u32[]{:S(2)}, u32[]{:S(2)}) collective-permute-start(bf16[520,128]{1,0:T(8,128)(2,1)S(1)} %collective-permute-done.9.rest_10_), channel_id=1, source_target_pairs={{0,1},{1,0},{2,3},{3,2},{4,5},{5,4},{6,7},{7,6},{8,9},{9,8},{10,11... | collective-permute-start | bytes 399368 | tf_op jit(solution)/shard_map/ppermute | solution.py:364
  18.9 10.8 %collective-permute-start.13 = (bf16[520,128]{1,0:T(8,128)(2,1)S(1)}, bf16[520,128]{1,0:T(8,128)(2,1)S(1)}, u32[]{:S(2)}, u32[]{:S(2)}) collective-permute-start(bf16[520,128]{1,0:T(8,128)(2,1)S(1)} %collective-permute-done.10.rest_0_), channel_id=1, source_target_pairs={{0,1},{1,0},{2,3},{3,2},{4,5},{5,4},{6,7},{7,6},{8,9},{9,8},{10,11... | collective-permute-start | bytes 399368 | tf_op jit(solution)/shard_map/ppermute | solution.py:364
  20.3 9.5 %collective-permute-start.14 = (bf16[520,128]{1,0:T(8,128)(2,1)S(1)}, bf16[520,128]{1,0:T(8,128)(2,1)S(1)}, u32[]{:S(2)}, u32[]{:S(2)}) collective-permute-start(bf16[520,128]{1,0:T(8,128)(2,1)S(1)} %collective-permute-done.12.rest_2_), channel_id=1, source_target_pairs={{0,1},{1,0},{2,3},{3,2},{4,5},{5,4},{6,7},{7,6},{8,9},{9,8},{10,11... | collective-permute-start | bytes 399368 | tf_op jit(solution)/shard_map/ppermute | solution.py:364
